TPU v7x, 128 devices: a whole 4x4x4 slice. The times are simulated.
128 devices in a mesh: rows: 32 (over y, x, core), cols: 4 (over z).
Axes of the slice: x: 4, y: 4, z: 4, core: 2. Of those that a mesh axis runs over, the one named last changes fastest.
Arguments:
- feats: bfloat16 [131072, 512], P('rows', 'cols'), may hold values from -6 to 6
- adj_vals: bfloat16 [1024, 16, 128, 128], P('rows'), may hold values from -0.125 to 0.125
- colref: int32 [1024, 16], P('rows'), may hold values from 0 to 95, as said below
- fetch_ids: int32 [32, 32, 2], P('rows'), may hold values from -1 to 31, as said below
- w_self: bfloat16 [512, 512], replicated, may hold values from -0.25 to 0.25
- w_neigh: bfloat16 [512, 512], replicated, may hold values from -0.25 to 0.25
- grad_out: bfloat16 [131072, 512], P(('rows', 'cols')), may hold values from -6 to 6
Outputs:
- act_out: bfloat16 [131072, 512], P(('rows', 'cols'))
- grad_self_w: float32 [512, 512], replicated
- grad_neigh_w: float32 [512, 512], replicated
- grad_feats: float32 [131072, 512], P('rows', 'cols')
Inputs may be any that keep to these rules, and one draw needn't show every extreme that they name: `fetch_ids`: entry [r, o, s] is a row tile index within partition o (0 to 31) that partition r reads, or -1 for an empty slot. The entries of one r and o are distinct, all slots with o = r are empty, and every r fills all 2 slots of at least one o. `colref`: entry [b, k], with r = b // 32, is below 32 for partition r's own row tile of that index, or 32 + o * 2 + s for the slot s of fetch_ids[r, o], never an empty slot; so it lies in 0 to 32 + 32 * 2 - 1. The 16 entries of a row tile are distinct and the first is b - r * 32, the row tile itself.
All inputs are finite; a program needn't handle non-finite values.
Results may differ from a plain program's by a relative error of at most 0.0057.
Values may be sent and summed in bfloat16 or wider, within the bound.
A program may use at most 192 MiB of HBM per device.

v0:
```python
import math

import jax
import jax.numpy as jnp
from jax import lax
from jax.sharding import PartitionSpec as P


def body(feats, adj_vals, colref, fetch_ids, w_self, w_neigh, grad_out):
    node_rows, feat_cols = feats.shape
    blocks = adj_vals.shape[0]
    per_block = adj_vals.shape[1]
    tile_rows = adj_vals.shape[2]
    partitions = lax.axis_size("rows")
    capacity = fetch_ids.shape[2]
    total_nodes = node_rows * partitions
    own_tiles = feats.reshape(blocks, tile_rows * feat_cols)
    wanted = lax.all_to_all(fetch_ids, "rows", split_axis=1, concat_axis=0, tiled=True).reshape(
        partitions * capacity
    )
    choose = (wanted[:, None] == jnp.arange(blocks, dtype=jnp.int32)[None, :]).astype(jnp.bfloat16)
    outgoing = jnp.dot(choose, own_tiles, preferred_element_type=jnp.float32).astype(jnp.bfloat16)
    outgoing = outgoing.reshape(partitions, capacity, tile_rows, feat_cols)
    arrived = lax.all_to_all(outgoing, "rows", split_axis=0, concat_axis=0, tiled=True)
    tile_pool = jnp.concatenate(
        [
            feats.reshape(blocks, tile_rows, feat_cols),
            arrived.reshape(partitions * capacity, tile_rows, feat_cols),
        ],
        axis=0,
    )
    picked = jnp.take(tile_pool, colref, axis=0)
    aggregated = jnp.einsum("bkij,bkjf->bif", adj_vals, picked, preferred_element_type=jnp.float32)
    aggregated = aggregated.astype(jnp.bfloat16).reshape(node_rows, feat_cols)
    feat_rows, agg_rows = (
        lax.all_to_all(feats, "cols", split_axis=0, concat_axis=1, tiled=True),
        lax.all_to_all(aggregated, "cols", split_axis=0, concat_axis=1, tiled=True),
    )
    preact = jnp.dot(feat_rows, w_self, preferred_element_type=jnp.float32) + jnp.dot(
        agg_rows, w_neigh, preferred_element_type=jnp.float32
    )
    activation, pull_back = jax.vjp(jax.nn.gelu, preact)
    grad_pre = pull_back(grad_out.astype(jnp.float32))[0].astype(jnp.bfloat16)
    contract = (((0,), (0,)), ((), ()))
    weight_terms = (
        lax.dot_general(feat_rows, grad_pre, contract, preferred_element_type=jnp.float32),
        lax.dot_general(agg_rows, grad_pre, contract, preferred_element_type=jnp.float32),
    )
    self_sum, neigh_sum = lax.psum((weight_terms[0], weight_terms[1]), ("rows", "cols"))
    grad_scale = 1.0 / math.sqrt(total_nodes)
    grad_self_w = self_sum * grad_scale
    grad_neigh_w = neigh_sum * grad_scale
    dims_back = (((1,), (1,)), ((), ()))
    column = lax.axis_index("cols") * feat_cols
    self_slice = lax.dynamic_slice_in_dim(w_self, column, feat_cols, 0)
    neigh_slice = lax.dynamic_slice_in_dim(w_neigh, column, feat_cols, 0)
    rows_in = lax.all_gather(grad_pre, "cols", axis=0, tiled=True)
    self_cols = lax.dot_general(rows_in, self_slice, dims_back, preferred_element_type=jnp.float32)
    neigh_cols = lax.dot_general(
        rows_in, neigh_slice, dims_back, preferred_element_type=jnp.float32
    )
    stacked = jnp.concatenate([self_cols, neigh_cols], axis=1).astype(jnp.bfloat16)
    self_part = stacked[:, :feat_cols]
    grad_agg = stacked[:, feat_cols:]
    grad_blocks = grad_agg.reshape(blocks, tile_rows, feat_cols)
    per_ref = jnp.einsum(
        "bkij,bif->bkjf", adj_vals, grad_blocks, preferred_element_type=jnp.float32
    )
    pool_slots = blocks + partitions * capacity
    pick_table = (
        jnp.arange(pool_slots, dtype=jnp.int32)[:, None] == colref.reshape(1, blocks * per_block)
    ).astype(jnp.float32)
    pooled = jnp.dot(
        pick_table,
        per_ref.reshape(blocks * per_block, tile_rows * feat_cols),
        precision=lax.Precision.HIGHEST,
        preferred_element_type=jnp.float32,
    )
    shares = pooled.astype(jnp.bfloat16).reshape(pool_slots, tile_rows, feat_cols)
    remote_shares = shares[blocks:].reshape(partitions, capacity, tile_rows, feat_cols)
    returned = lax.all_to_all(remote_shares, "rows", split_axis=0, concat_axis=0, tiled=True)
    gathered_back = jnp.dot(
        choose.T,
        returned.reshape(partitions * capacity, tile_rows * feat_cols),
        preferred_element_type=jnp.float32,
    )
    grad_feats = self_part.astype(jnp.float32) + shares[:blocks].astype(jnp.float32).reshape(
        node_rows, feat_cols
    )
    grad_feats = grad_feats + gathered_back.reshape(node_rows, feat_cols)
    return (activation.astype(jnp.bfloat16), grad_self_w, grad_neigh_w, grad_feats)


def solution(mesh):
    in_specs = (
        P("rows", "cols"),
        P("rows", None, None, None),
        P("rows", None),
        P("rows", None, None),
        P(),
        P(),
        P(("rows", "cols"), None),
    )
    out_specs = (P(("rows", "cols"), None), P(), P(), P("rows", "cols"))
    return jax.shard_map(body, mesh=mesh, in_specs=in_specs, out_specs=out_specs, check_vma=False)
```

profile of v0, /device:TPU:1, one launch (start us, length us, event | category | flops | bytes accessed | tf_op | source)
XLA Modules:
  0.0 467.5 jit_solution(2527435484349896378)
XLA Ops:
  8.0 0.0 copy-start
  8.0 1.4 copy.40
  9.4 8.6 %all-to-all-start.1 = ((s32[1,32,2]{2,0,1:T(1,128)}), s32[1,32,2]{2,0,1:T(1,128)S(1)}, u32[]{:S(2)}, u32[]{:S(2)}) async-start(s32[1,32,2]{2,0,1:T(1,128)} %copy.40), calls=%async_computation.1 | async-start | bytes 32768 | tf_op jit(solution)/shard_map/all_to_all | solution.py:18
  18.0 1.5 reshape.64
  19.6 5.3 %all-to-all-done.1 = s32[1,32,2]{2,0,1:T(1,128)S(1)} async-done(((s32[1,32,2]{2,0,1:T(1,128)}), s32[1,32,2]{2,0,1:T(1,128)S(1)}, u32[]{:S(2)}, u32[]{:S(2)}) %all-to-all-start.1) | async-done | bytes 288 | tf_op jit(solution)/shard_map/all_to_all | solution.py:18
  24.9 0.5 broadcast.41
  25.4 0.7 reduce.3
  26.1 0.1 eq.30
  26.2 0.8 fusion.28
  27.0 1.9 copy.54
  28.9 0.0 copy-start.6
  28.9 4.4 all-to-all-start.2
  33.3 0.0 copy-done.6
  33.3 0.1 copy.41
  33.4 0.1 reshape.75
  33.5 0.1 copy.39
  33.6 27.7 %all-to-all-done.2 = bf16[32,2,128,128]{3,2,1,0:T(8,128)(2,1)S(1)} async-done(((bf16[32,2,128,128]{3,2,1,0:T(8,128)(2,1)}), bf16[32,2,128,128]{3,2,1,0:T(8,128)(2,1)S(1)}, u32[]{:S(2)}, u32[]{:S(2)}) %all-to-all-start.2) | async-done | bytes 2097184 | tf_op jit(solution)/shard_map/all_to_all | solution.py:24
  61.3 5.0 %all-to-all-start = ((bf16[4,1024,128]{2,1,0:T(8,128)(2,1)}), bf16[4,1024,128]{2,1,0:T(8,128)(2,1)}, u32[]{:S(2)}, u32[]{:S(2)}) async-start(bf16[4,1024,128]{2,1,0:T(8,128)(2,1)} %bitcast), calls=%async_computation | async-start | bytes 2097152 | tf_op jit(solution)/shard_map/all_to_all | solution.py:36
  66.3 3.2 pad_maximum_fusion
  69.5 15.8 %gather_fusion = bf16[512,128,128]{2,1,0:T(8,128)(2,1)} fusion(bf16[96,128,128]{2,1,0:T(8,128)(2,1)} %pad_maximum_fusion, s32[1024]{0:T(1024)S(1)} %pad_clamp_fusion), kind=kCustom, calls=%fused_computation | custom fusion | bytes 33556480 | tf_op jit(solution)/shard_map/jit(_take)/gather | solution.py:32
  85.3 13.0 %bitcast_convert_fusion = bf16[32,128,128]{1,2,0:T(8,128)(2,1)S(1)} fusion(bf16[32,16,128,128]{3,2,1,0:T(8,128)(2,1)} %param.8, bf16[32,16,128,128]{3,2,1,0:T(8,128)(2,1)} %bitcast.60, pred[32,16]{1,0:T(8,128)(4,1)S(1)} %copy.39), kind=kOutput, calls=%fused_computation.35 | convolution fusion | flops 2156396544 | bytes 34603520 | tf_op jit(solution)/shard_map/bkij,bkjf->bif/dot_general | solution.py:33
  98.3 1.3 copy.42
  99.6 0.0 copy-start.5
  99.6 0.0 all-to-all-done
  99.6 4.4 all-to-all-start.3
  104.0 0.0 all-reduce.3.cloned.1.call-start
  104.0 1.5 copy.38
  105.5 0.0 copy-done.5
  105.5 2.1 fusion.37
  107.6 8.0 %all-to-all-done.3 = bf16[4,1024,128]{1,2,0:T(8,128)(2,1)S(1)} async-done(((bf16[4,1024,128]{1,2,0:T(8,128)(2,1)}), bf16[4,1024,128]{1,2,0:T(8,128)(2,1)S(1)}, u32[]{:S(2)}, u32[]{:S(2)}) %all-to-all-start.3) | async-done | bytes 1048608 | tf_op jit(solution)/shard_map/all_to_all | solution.py:37
  115.6 0.0 copy-start.3
  115.6 1.0 copy-done.3
  116.6 0.0 copy-done
  116.6 5.4 %fusion.15 = (bf16[1024,512]{1,0:T(8,128)(2,1)S(1)}, bf16[1024,512]{1,0:T(8,128)(2,1)}) fusion(bf16[1024,512]{1,0:T(8,128)(2,1)} %param.13, f32[1024,512]{1,0:T(8,128)} %fusion.37, bf16[1024,512]{0,1:T(8,128)(2,1)} %bitcast.66, bf16[512,512]{1,0:T(8,128)(2,1)S(1)} %copy-done), kind=kOutput, calls=%fused_computation.23 | convolution fusion | flops 549453824 | bytes 6815744 | tf_op jit(solution)/shard_map/dot_general | solution.py:39
  122.0 0.0 copy-start.2
  122.0 0.0 copy-start.4
  122.0 1.7 convolution_bitcast_fusion.1
  123.7 0.0 copy-done.4
  123.7 1.7 fusion.38
  125.4 0.0 copy-done.2
  125.5 0.0 all-reduce.3.cloned.1.call-update
  125.5 0.0 all-gather.2.cloned.1.call-start
  125.5 0.5 all-gather.2.cloned.1.call-update
  126.1 0.1 copy.44
  126.1 0.1 eq.35
  126.2 178.1 %all-reduce.3.cloned.1.call-done = (f32[512,512]{0,1:T(8,128)}, f32[512,512]{0,1:T(8,128)}) async-done(((f32[512,512]{0,1:T(8,128)}, f32[512,512]{0,1:T(8,128)}), (f32[512,512]{0,1:T(8,128)}, f32[512,512]{0,1:T(8,128)})) %all-reduce.3.cloned.1.call-update) | async-done | bytes 2097168 | tf_op jit(solution)/shard_map/psum | solution.py:49
  304.3 1.8 broadcast_multiply_fusion
  306.1 1.3 copy.47
  307.4 1.3 copy.48
  308.7 0.0 all-gather.2.cloned.1.call-done
  308.7 3.4 convolution_convert_fusion.1
  312.2 21.4 %convolution_bitcast_fusion = f32[32,16,128,128]{2,3,1,0:T(8,128)} fusion(bf16[32,128,128,1]{2,1,3,0:T(8,128)(2,1)S(1)} %bitcast.63, bf16[32,16,128,128]{3,2,1,0:T(8,128)(2,1)} %param.8), kind=kOutput, calls=%fused_computation.9 | convolution fusion | flops 2147483648 | bytes 51380224 | tf_op jit(solution)/shard_map/bkij,bif->bkjf/dot_general | solution.py:66
  333.6 33.4 %copy.46 = f32[32,16,128,128]{3,2,1,0:T(8,128)} copy(f32[32,16,128,128]{2,3,1,0:T(8,128)} %convolution_bitcast_fusion) | data formatting | bytes 67108864 | tf_op jit(solution)/shard_map/bkij,bif->bkjf/dot_general | solution.py:66
  367.0 42.4 %fusion.3 = bf16[96,16384]{1,0:T(8,128)(2,1)} fusion(f32[64,8,128,128]{3,2,1,0:T(8,128)} %bitcast.59, s32[512]{0:T(512)S(1)} %eq.35), kind=kOutput, calls=%fused_computation.4 | convolution fusion | flops 9665298432 | bytes 36702208 | tf_op jit(solution)/shard_map/dot_general | solution.py:73
  409.4 1.7 slice_bitcast_fusion
  411.1 1.9 copy.56
  413.0 6.5 %all-to-all-start.4 = ((bf16[32,2,128,128]{3,2,1,0:T(8,128)(2,1)}), bf16[32,2,128,128]{3,2,1,0:T(8,128)(2,1)}, u32[]{:S(2)}, u32[]{:S(2)}) async-start(bf16[32,2,128,128]{3,2,1,0:T(8,128)(2,1)} %bitcast.29), calls=%async_computation.4 | async-start | bytes 4194304 | tf_op jit(solution)/shard_map/all_to_all | solution.py:81
  419.6 2.7 slice_convert_fusion
  422.2 1.7 reshape.72
  423.9 23.5 %all-to-all-done.4 = bf16[32,2,128,128]{3,2,1,0:T(8,128)(2,1)} async-done(((bf16[32,2,128,128]{3,2,1,0:T(8,128)(2,1)}), bf16[32,2,128,128]{3,2,1,0:T(8,128)(2,1)}, u32[]{:S(2)}, u32[]{:S(2)}) %all-to-all-start.4) | async-done | bytes 2097184 | tf_op jit(solution)/shard_map/all_to_all | solution.py:81
  447.4 4.4 fusion.23
  451.8 2.7 reshape.71
  454.6 5.5 %fusion.12 = f32[4096,128]{1,0:T(8,128)} fusion(f32[4096,128]{1,0:T(8,128)} %reshape.71, f32[4096,128]{1,0:T(8,128)S(1)} %reshape.72, bf16[4096,512]{1,0:T(8,128)(2,1)} %all-gather.2.cloned.1.call-done, bf16[512,512]{1,0:T(8,128)(2,1)S(1)} %copy-done.5, s32[]{:T(128)S(6)} %select_n.15), kind=kOutput, calls=%fused_computation.15 | convolution fusion | flops 538968064 | bytes 10616836 | tf_op jit(solution)/shard_map/dot_general | solution.py:58
  460.1 0.0 copy-done.1
  (4 shorter events, 0.0 us)
Async XLA Ops:
  8.0 108.6 %copy-start = (bf16[512,512]{1,0:T(8,128)(2,1)S(1)}, bf16[512,512]{1,0:T(8,128)(2,1)}, u32[]{:S(2)}) copy-start(bf16[512,512]{1,0:T(8,128)(2,1)} %param.12) | copy-start | bytes 1572868
  9.4 15.5 %all-to-all-start.1 = ((s32[1,32,2]{2,0,1:T(1,128)}), s32[1,32,2]{2,0,1:T(1,128)S(1)}, u32[]{:S(2)}, u32[]{:S(2)}) async-start(s32[1,32,2]{2,0,1:T(1,128)} %copy.40), calls=%async_computation.1 | async-start | bytes 32768 | tf_op jit(solution)/shard_map/all_to_all | solution.py:18
  28.9 4.5 copy-start.6
  28.9 32.4 %all-to-all-start.2 = ((bf16[32,2,128,128]{3,2,1,0:T(8,128)(2,1)}), bf16[32,2,128,128]{3,2,1,0:T(8,128)(2,1)S(1)}, u32[]{:S(2)}, u32[]{:S(2)}) async-start(bf16[32,2,128,128]{3,2,1,0:T(8,128)(2,1)} %bitcast.62), calls=%async_computation.2 | async-start | bytes 4194304 | tf_op jit(solution)/shard_map/all_to_all | solution.py:24
  61.3 38.3 %all-to-all-start = ((bf16[4,1024,128]{2,1,0:T(8,128)(2,1)}), bf16[4,1024,128]{2,1,0:T(8,128)(2,1)}, u32[]{:S(2)}, u32[]{:S(2)}) async-start(bf16[4,1024,128]{2,1,0:T(8,128)(2,1)} %bitcast), calls=%async_computation | async-start | bytes 2097152 | tf_op jit(solution)/shard_map/all_to_all | solution.py:36
  99.6 5.9 %copy-start.5 = (bf16[512,512]{1,0:T(8,128)(2,1)S(1)}, bf16[512,512]{1,0:T(8,128)(2,1)}, u32[]{:S(2)}) copy-start(bf16[512,512]{1,0:T(8,128)(2,1)} %param.11) | copy-start | bytes 1572868
  99.6 16.0 %all-to-all-start.3 = ((bf16[4,1024,128]{1,2,0:T(8,128)(2,1)}), bf16[4,1024,128]{1,2,0:T(8,128)(2,1)S(1)}, u32[]{:S(2)}, u32[]{:S(2)}) async-start(bf16[4,1024,128]{1,2,0:T(8,128)(2,1)} %copy.42), calls=%async_computation.3 | async-start | bytes 2097152 | tf_op jit(solution)/shard_map/all_to_all | solution.py:37
  104.0 200.3 %all-reduce.3.cloned.1.call-start = ((), (), s32[]{:S(2)}) async-start(), calls=%async_computation.6 | async-start | bytes 4194304 | tf_op jit(solution)/shard_map/psum | solution.py:49
  115.6 1.0 copy-start.3
  122.0 3.5 copy-start.2
  122.0 1.7 copy-start.4
  125.5 183.3 %all-gather.2.cloned.1.call-start = ((), (), s32[]{:S(2)}) async-start(), calls=%async_computation.5 | async-start | bytes 5242880 | tf_op jit(solution)/shard_map/all_gather | solution.py:57
  413.0 34.4 %all-to-all-start.4 = ((bf16[32,2,128,128]{3,2,1,0:T(8,128)(2,1)}), bf16[32,2,128,128]{3,2,1,0:T(8,128)(2,1)}, u32[]{:S(2)}, u32[]{:S(2)}) async-start(bf16[32,2,128,128]{3,2,1,0:T(8,128)(2,1)} %bitcast.29), calls=%async_computation.4 | async-start | bytes 4194304 | tf_op jit(solution)/shard_map/all_to_all | solution.py:81
  454.6 5.5 %copy-start.1 = (bf16[512,512]{1,0:T(8,128)(2,1)S(1)}, bf16[512,512]{1,0:T(8,128)(2,1)}, u32[]{:S(2)}) copy-start(bf16[512,512]{1,0:T(8,128)(2,1)} %param.12) | copy-start | bytes 1572868
Sparse Core Ops, SparseCore 0:
  125.6 178.6 all-reduce.2
Sparse Core Ops, SparseCore 1:
  128.2 50.6 all-gather.1
where the time goes:
time: 470 us; the launch traced here: 468 us
  waiting for transfers between devices  243 us (52%)
  matrix products  102 us (22%)
  local copies, waits for them, and re-layouts  69.6 us (15%)
  starting transfers between devices  29 us (6%)
  between operations  15.6 us (3%)
  other arithmetic  8.32 us (2%)
    psum x1, waiting for transfers between devices, body(): lax.psum((weight_terms[0], weight_terms[1]), ('rows', 'cols'))  178 us
    dot_general x1, matrix products, body(): jnp.dot(pick_table, per_ref.reshape(blocks * per_block, tile_rows * feat_...  42.4 us
    dot_general x1, local copies, waits for them, and re-layouts, body(): jnp.einsum('bkij,bif->bkjf', adj_vals, grad_blocks, preferred_element_typ...  33.4 us
    all_to_all x1, waiting for transfers between devices, body(): lax.all_to_all(outgoing, 'rows', split_axis=0, concat_axis=0, tiled=True)  27.7 us
    all_to_all x1, waiting for transfers between devices, body(): lax.all_to_all(remote_shares, 'rows', split_axis=0, concat_axis=0, tiled=...  23.5 us
    dot_general x1, matrix products, body(): jnp.einsum('bkij,bif->bkjf', adj_vals, grad_blocks, preferred_element_typ...  21.4 us
    gather x1, local copies, waits for them, and re-layouts, body(): picked = jnp.take(tile_pool, colref, axis=0)  15.8 us
    dot_general x1, matrix products, body(): jnp.einsum('bkij,bkjf->bif', adj_vals, picked, preferred_element_type=jnp...  13 us
  transfers between devices with their start and end apart: 7, of which 5 were waited for; matrix products, arithmetic and copies ran while one was open for 10% of the time, Pallas kernels for 0%

commit v1 on v0

v1 whole, which is shorter than its diff:
```python
import functools
import math

import jax
import jax.numpy as jnp
from jax import lax
from jax.experimental import pallas as pl
from jax.experimental.pallas import tpu as pltpu
from jax.sharding import PartitionSpec as P

MESH = pl.DeviceIdType.MESH
ANY = pl.BlockSpec(memory_space=pl.ANY)
VMEM = pl.BlockSpec(memory_space=pltpu.VMEM)
SMEM = pl.BlockSpec(memory_space=pltpu.SMEM)
BF16 = jnp.bfloat16
F32 = jnp.float32


def remote(src, dst, send, recv, axis, peer):
    return pltpu.make_async_remote_copy(
        src_ref=src, dst_ref=dst, send_sem=send, recv_sem=recv,
        device_id={axis: peer}, device_id_type=MESH,
    )


def forward_kernel(parts, cols, cap, blocks, per_block, fetch_ref, colref_ref, feats_hbm, adj_hbm,
                   frows_hbm, arows_hbm, wanted_ref,
                   pool, own_v, adj_v, stage, agg_v, idx_v, idx_s,
                   pool_sem, adj_sem, own_sem, ownv_sem, smem_sem,
                   idx_send, idx_recv, tile_send, tile_recv, f_send, f_recv, a_send, a_recv):
    me = lax.axis_index("rows")
    mc = lax.axis_index("cols")
    share = blocks // cols

    pltpu.make_async_copy(feats_hbm, own_v, ownv_sem).start()
    pltpu.make_async_copy(feats_hbm, pool.at[pl.ds(0, blocks)], pool_sem).start()
    for q in range(cols):
        pltpu.make_async_copy(adj_hbm.at[pl.ds(q * share, share)], adj_v.at[pl.ds(q * share, share)], adj_sem.at[q]).start()

    barrier = pltpu.get_barrier_semaphore()

    def hello(d, _):
        pl.semaphore_signal(barrier, inc=1, device_id={"rows": lax.rem(me + d, parts)}, device_id_type=MESH)
        return 0

    lax.fori_loop(1, parts, hello, 0)
    for d in range(1, cols):
        pl.semaphore_signal(barrier, inc=1, device_id={"cols": lax.rem(mc + d, cols)}, device_id_type=MESH)
    pl.semaphore_wait(barrier, parts - 1 + cols - 1)

    def ask(d, _):
        p = lax.rem(me + d, parts)
        remote(fetch_ref.at[p], idx_v.at[me], idx_send.at[p], idx_recv.at[me], "rows", p).start()
        return 0

    lax.fori_loop(1, parts, ask, 0)
    idx_v[me] = jnp.full(idx_v.shape[1:], -1, jnp.int32)

    for d in range(1, cols):
        p = lax.rem(mc + d, cols)
        remote(feats_hbm.at[pl.ds(p * share, share)], frows_hbm.at[mc], f_send.at[p], f_recv.at[mc], "cols", p).start()
    own = pltpu.make_async_copy(feats_hbm.at[pl.ds(mc * share, share)], frows_hbm.at[mc], own_sem)
    own.start()

    pltpu.make_async_copy(feats_hbm, own_v, ownv_sem).wait()

    def asked(d, _):
        p = lax.rem(me + parts - d, parts)
        remote(fetch_ref.at[p], idx_v.at[p], idx_send.at[p], idx_recv.at[p], "rows", p).wait_recv()
        return 0

    lax.fori_loop(1, parts, asked, 0)
    to_smem = pltpu.make_async_copy(idx_v, idx_s, smem_sem)
    to_smem.start()
    to_smem.wait()
    wanted_ref[...] = idx_v[...]

    def give(d, _):
        p = lax.rem(me + d, parts)
        for s in range(cap):
            stage[p, s] = own_v[jnp.maximum(idx_s[p, 0, s], 0)]
        remote(stage.at[p], pool.at[pl.ds(blocks + me * cap, cap)], tile_send.at[p], tile_recv.at[me], "rows", p).start()
        return 0

    lax.fori_loop(1, parts, give, 0)
    pool[pl.ds(blocks + me * cap, cap)] = jnp.zeros((cap,) + pool.shape[1:], BF16)
    pltpu.make_async_copy(feats_hbm, pool.at[pl.ds(0, blocks)], pool_sem).wait()
    for q in range(cols):
        pltpu.make_async_copy(adj_hbm.at[pl.ds(q * share, share)], adj_v.at[pl.ds(q * share, share)], adj_sem.at[q]).wait()

    def given(d, _):
        p = lax.rem(me + parts - d, parts)
        remote(stage.at[p], pool.at[pl.ds(blocks + p * cap, cap)], tile_send.at[p], tile_recv.at[p], "rows", p).wait_recv()
        return 0

    lax.fori_loop(1, parts, given, 0)

    def aggregate(b):
        left = jnp.concatenate([adj_v[b, k] for k in range(per_block)], axis=1)
        right = jnp.concatenate([pool[colref_ref[b * per_block + k]] for k in range(per_block)], axis=0)
        return jnp.dot(left, right, preferred_element_type=F32).astype(BF16)

    def tile_round(i, _):
        def one(d, _):
            p = lax.rem(mc + d, cols)
            agg_v[p, i] = aggregate(p * share + i)
            remote(agg_v.at[p, i], arows_hbm.at[mc, i], a_send.at[p, i], a_recv.at[mc, i], "cols", p).start()
            return 0

        lax.fori_loop(1, cols, one, 0)
        agg_v[mc, i] = aggregate(mc * share + i)
        return 0

    lax.fori_loop(0, share, tile_round, 0)
    own_agg = pltpu.make_async_copy(agg_v.at[mc], arows_hbm.at[mc], pool_sem)
    own_agg.start()

    for d in range(1, cols):
        p = lax.rem(mc + d, cols)
        remote(feats_hbm.at[pl.ds(p * share, share)], frows_hbm.at[p], f_send.at[p], f_recv.at[p], "cols", p).wait()
    own.wait()
    own_agg.wait()

    def drain(d, _):
        p = lax.rem(me + d, parts)
        remote(fetch_ref.at[p], idx_v.at[p], idx_send.at[p], idx_recv.at[p], "rows", p).wait_send()
        remote(stage.at[p], pool.at[pl.ds(blocks + p * cap, cap)], tile_send.at[p], tile_recv.at[p], "rows", p).wait_send()
        return 0

    lax.fori_loop(1, parts, drain, 0)

    def drain_agg(i, _):
        for d in range(1, cols):
            p = lax.rem(mc + d, cols)
            remote(agg_v.at[p, i], arows_hbm.at[p, i], a_send.at[p, i], a_recv.at[p, i], "cols", p).wait()
        return 0

    lax.fori_loop(0, share, drain_agg, 0)


def forward(fetch, colref, feats, adj, parts, cols, cap):
    blocks, per_block, tile, _ = adj.shape
    width = feats.shape[-1]
    share = blocks // cols
    DMA = pltpu.SemaphoreType.DMA
    rows_shape = jax.ShapeDtypeStruct((cols, share, tile, width), BF16)
    return pl.pallas_call(
        functools.partial(forward_kernel, parts, cols, cap, blocks, per_block),
        out_shape=(rows_shape, rows_shape, jax.ShapeDtypeStruct(fetch.shape, jnp.int32)),
        in_specs=[VMEM, SMEM, ANY, ANY],
        out_specs=(ANY, ANY, VMEM),
        scratch_shapes=[
            pltpu.VMEM((blocks + parts * cap, tile, width), BF16),
            pltpu.VMEM(feats.shape, BF16),
            pltpu.VMEM(adj.shape, BF16),
            pltpu.VMEM((parts, cap, tile, width), BF16),
            pltpu.VMEM((cols, share, tile, width), BF16),
            pltpu.VMEM(fetch.shape, jnp.int32),
            pltpu.SMEM(fetch.shape, jnp.int32),
            DMA, DMA((cols,)), DMA, DMA, DMA,
            DMA((parts,)), DMA((parts,)), DMA((parts,)), DMA((parts,)),
            DMA((cols,)), DMA((cols,)), DMA((cols, share)), DMA((cols, share)),
        ],
        compiler_params=pltpu.CompilerParams(collective_id=0, has_side_effects=True, vmem_limit_bytes=48 << 20),
        name="forward",
    )(fetch, colref, feats, adj)


def dense_kernel(scale, frows_ref, arows_ref, wself_ref, wneigh_ref, gout_ref,
                 act_ref, back_ref, gw_ref):
    cols, step, tile, width = frows_ref.shape
    hid = cols * width
    rows = step * tile
    step_id = pl.program_id(0)

    def rows_of(ref):
        return jnp.concatenate([ref[c].reshape(rows, width) for c in range(cols)], axis=1)

    both = jnp.concatenate([rows_of(frows_ref), rows_of(arows_ref)], axis=1)
    wself, wneigh = wself_ref[...], wneigh_ref[...]
    v = jnp.dot(both, jnp.concatenate([wself, wneigh], axis=0), preferred_element_type=F32)
    c0 = math.sqrt(2.0 / math.pi)
    v2 = v * v
    t = jnp.tanh(c0 * v * (1.0 + 0.044715 * v2))
    half = 0.5 * (1.0 + t)
    act_ref[...] = (v * half).astype(BF16)
    slope = half + (0.5 * v) * (1.0 - t * t) * (c0 * (1.0 + 3.0 * 0.044715 * v2))
    grad_pre = (gout_ref[...].astype(F32) * slope).astype(BF16)
    nt = (((1,), (1,)), ((), ()))
    for n, w in enumerate((wneigh, wself)):
        out = lax.dot_general(grad_pre, w, nt, preferred_element_type=F32).astype(BF16)
        for c in range(cols):
            back_ref[c, n] = out[:, c * width:(c + 1) * width].reshape(step, tile, width)
    gw = lax.dot_general(both, grad_pre, (((0,), (0,)), ((), ())), preferred_element_type=F32)

    @pl.when(step_id == 0)
    def _():
        gw_ref[...] = gw

    @pl.when(step_id > 0)
    def _():
        gw_ref[...] += gw

    @pl.when(step_id == pl.num_programs(0) - 1)
    def _():
        gw_ref[...] = gw_ref[...] * scale


def dense(frows, arows, wself, wneigh, gout, scale):
    cols, share, tile, width = frows.shape
    hid = cols * width
    step = 2
    block = pl.BlockSpec((cols, step, tile, width), lambda i: (0, i, 0, 0))
    whole = pl.BlockSpec((hid, hid), lambda i: (0, 0))
    rows = pl.BlockSpec((step * tile, hid), lambda i: (i, 0))
    return pl.pallas_call(
        functools.partial(dense_kernel, scale),
        grid=(share // step,),
        out_shape=(
            jax.ShapeDtypeStruct(gout.shape, BF16),
            jax.ShapeDtypeStruct((cols, 2, share, tile, width), BF16),
            jax.ShapeDtypeStruct((2 * hid, hid), F32),
        ),
        in_specs=[block, block, whole, whole, rows],
        out_specs=(
            rows,
            pl.BlockSpec((cols, 2, step, tile, width), lambda i: (0, 0, i, 0, 0)),
            pl.BlockSpec((2 * hid, hid), lambda i: (0, 0)),
        ),
        compiler_params=pltpu.CompilerParams(vmem_limit_bytes=48 << 20),
        name="dense",
    )(frows, arows, wself, wneigh, gout)


def spread_kernel(per_step, colref_ref, adj_ref, gagg_ref, own_ref, share_ref, pool):
    step_id = pl.program_id(0)
    blocks = own_ref.shape[0]
    per_block = adj_ref.shape[1]
    width = pool.shape[1]

    @pl.when(step_id == 0)
    def _():
        pool[...] = jnp.zeros_like(pool)

    for j in range(per_step):
        b = step_id * per_step + j
        grad_t = gagg_ref[j].T
        for k in range(0, per_block, 2):
            pair = jnp.concatenate([adj_ref[j, k], adj_ref[j, k + 1]], axis=1)
            out = jnp.dot(grad_t, pair, preferred_element_type=F32)
            half = out.shape[1] // 2
            pool[colref_ref[b * per_block + k]] += out[:, :half]
            pool[colref_ref[b * per_block + k + 1]] += out[:, half:]

    @pl.when(step_id == pl.num_programs(0) - 1)
    def _():
        def own(t, _):
            own_ref[t] = pool[t].astype(BF16).T
            return 0

        def away(t, _):
            share_ref[t] = pool[blocks + t].astype(BF16).T
            return 0

        lax.fori_loop(0, blocks, own, 0, unroll=4)
        lax.fori_loop(0, share_ref.shape[0], away, 0, unroll=4)


def spread(colref, adj, gagg, slots):
    blocks, per_block, tile, _ = adj.shape
    width = gagg.shape[-1]
    per_step = 4
    return pl.pallas_call(
        functools.partial(spread_kernel, per_step),
        grid=(blocks // per_step,),
        out_shape=(
            jax.ShapeDtypeStruct((blocks, tile, width), BF16),
            jax.ShapeDtypeStruct((slots, tile, width), BF16),
        ),
        in_specs=[
            SMEM,
            pl.BlockSpec((per_step, per_block, tile, tile), lambda i: (i, 0, 0, 0)),
            pl.BlockSpec((per_step, tile, width), lambda i: (i, 0, 0)),
        ],
        out_specs=(
            pl.BlockSpec((blocks, tile, width), lambda i: (0, 0, 0)),
            pl.BlockSpec((slots, tile, width), lambda i: (0, 0, 0)),
        ),
        scratch_shapes=[pltpu.VMEM((blocks + slots, width, tile), F32)],
        compiler_params=pltpu.CompilerParams(vmem_limit_bytes=48 << 20),
        name="spread",
    )(colref, adj, gagg)


def combine_kernel(wanted_ref, self_ref, own_ref, back_ref, out_ref):
    slots = back_ref.shape[0]
    out_ref[...] = self_ref[...].astype(F32) + own_ref[...].astype(F32)

    def add(s, _):
        t = wanted_ref[s]

        @pl.when(t >= 0)
        def _():
            out_ref[t] += back_ref[s].astype(F32)

        return 0

    lax.fori_loop(0, slots, add, 0)


def combine(wanted, self_part, own, back):
    return pl.pallas_call(
        combine_kernel,
        out_shape=jax.ShapeDtypeStruct(own.shape, F32),
        in_specs=[SMEM, VMEM, VMEM, VMEM],
        out_specs=VMEM,
        compiler_params=pltpu.CompilerParams(vmem_limit_bytes=48 << 20),
        name="combine",
    )(wanted, self_part, own, back)


def body(feats, adj_vals, colref, fetch_ids, w_self, w_neigh, grad_out):
    node_rows, width = feats.shape
    blocks, per_block, tile, _ = adj_vals.shape
    parts = lax.axis_size("rows")
    cols = lax.axis_size("cols")
    cap = fetch_ids.shape[2]
    slots = parts * cap
    hid = width * cols
    scale = 1.0 / math.sqrt(node_rows * parts)
    fetch = jnp.pad(fetch_ids.reshape(parts, 1, cap), ((0, 0), (0, 0), (0, 128 - cap)))
    refs = colref.reshape(blocks * per_block)
    frows, arows, wanted = forward(fetch, refs, feats.reshape(blocks, tile, width), adj_vals, parts, cols, cap)
    act, back, gw = dense(frows, arows, w_self, w_neigh, grad_out, scale)
    back = lax.all_to_all(back, "cols", split_axis=0, concat_axis=0, tiled=True)
    gagg = back[:, 0].reshape(blocks, tile, width)
    self_part = back[:, 1].reshape(blocks, tile, width)
    own, shares = spread(refs, adj_vals, gagg, slots)
    returned = lax.all_to_all(shares.reshape(parts, cap, tile, width), "rows", split_axis=0, concat_axis=0, tiled=True)
    pieces = lax.all_to_all(
        gw.astype(BF16).reshape(parts, 2 * hid // parts, hid), "rows", split_axis=0, concat_axis=0, tiled=True
    )
    piece = lax.psum(pieces.astype(F32).sum(axis=0), "cols")
    sums = lax.all_gather(piece, "rows", axis=0, tiled=True)
    grad_feats = combine(wanted[:, 0, :cap].reshape(slots), self_part, own, returned.reshape(slots, tile, width))
    return act, sums[:hid], sums[hid:], grad_feats.reshape(node_rows, width)


def solution(mesh):
    in_specs = (
        P("rows", "cols"),
        P("rows", None, None, None),
        P("rows", None),
        P("rows", None, None),
        P(),
        P(),
        P(("rows", "cols"), None),
    )
    out_specs = (P(("rows", "cols"), None), P(), P(), P("rows", "cols"))
    return jax.shard_map(body, mesh=mesh, in_specs=in_specs, out_specs=out_specs, check_vma=False)
```

time: 470 us -> 238 us (0.51)
  waiting for transfers between devices: 243 us -> 63 us
  matrix products: 102 us -> 0 us
  Pallas kernels: 0 us -> 86.6 us
  local copies, waits for them, and re-layouts: 69.6 us -> 9.73 us
  blocking collectives: 0 us -> 49.5 us
  starting transfers between devices: 29 us -> 11 us
  other arithmetic: 8.32 us -> 2.51 us
    psum x1, waiting for transfers between devices: 178 us -> 35.2 us  [body(): piece = lax.psum(pieces.astype(F32).sum(axis=0), 'cols')]
    dot_general x11 -> x0, matrix products: 102 us -> none  [the longest x1 42.4 us: body(): jnp.dot(pick_table, per_ref.reshape(blocks * per_block, tile_rows * feat_...]
    pallas_call x0 -> x4, Pallas kernels: none -> 86.6 us  [the longest x1 61.6 us: forward(): pl.pallas_call(functools.partial(forward_kernel, parts, cols, cap, blocks...]
    all_to_all x0 -> x2, blocking collectives: none -> 49.5 us  [the longest x1 26.5 us: body(): back = lax.all_to_all(back, 'cols', split_axis=0, concat_axis=0, tiled=True)]
    all_to_all x5 -> x1, waiting for transfers between devices: 64.6 us -> 27.7 us  [body(): lax.all_to_all(shares.reshape(parts, cap, tile, width), 'rows', split_axi...]
    dot_general x1 -> x0, local copies, waits for them, and re-layouts: 33.4 us -> none  [body(): jnp.einsum('bkij,bif->bkjf', adj_vals, grad_blocks, preferred_element_typ...]
    all_to_all x5 -> x1, starting transfers between devices: 28.9 us -> 10.9 us  [body(): lax.all_to_all(shares.reshape(parts, cap, tile, width), 'rows', split_axi...]
    gather x1 -> x0, local copies, waits for them, and re-layouts: 15.8 us -> none  [body(): picked = jnp.take(tile_pool, colref, axis=0)]
  transfers between devices with their start and end apart: 7 -> 3, of which waited for: 5 -> 2; matrix products, arithmetic and copies ran while one was open for 10% -> 0% of each run, Pallas kernels for 0% -> 7%
where the time goes in v1:
time: 238 us; the launch traced here: 236 us
  Pallas kernels  86.6 us (36%)
  waiting for transfers between devices  63 us (26%)
  blocking collectives  49.5 us (21%)
  between operations  14.1 us (6%)
  starting transfers between devices  11 us (5%)
  local copies, waits for them, and re-layouts  9.73 us (4%)
  other arithmetic  2.51 us (1%)
    pallas_call x1, Pallas kernels, forward(): pl.pallas_call(functools.partial(forward_kernel, parts, cols, cap, blocks...  61.6 us
    psum x1, waiting for transfers between devices, body(): piece = lax.psum(pieces.astype(F32).sum(axis=0), 'cols')  35.2 us
    all_to_all x1, waiting for transfers between devices, body(): lax.all_to_all(shares.reshape(parts, cap, tile, width), 'rows', split_axi...  27.7 us
    all_to_all x1, blocking collectives, body(): back = lax.all_to_all(back, 'cols', split_axis=0, concat_axis=0, tiled=True)  26.5 us
    all_to_all x1, blocking collectives, body(): lax.all_to_all(gw.astype(BF16).reshape(parts, 2 * hid // parts, hid), 'ro...  22.9 us
    pallas_call x1, Pallas kernels, spread(): pl.pallas_call(functools.partial(spread_kernel, per_step), grid=(blocks /...  13.6 us
    all_to_all x1, starting transfers between devices, body(): lax.all_to_all(shares.reshape(parts, cap, tile, width), 'rows', split_axi...  10.9 us
    pallas_call x1, Pallas kernels, dense(): pl.pallas_call(functools.partial(dense_kernel, scale), grid=(share // ste...  8.21 us
  transfers between devices with their start and end apart: 3, of which 2 were waited for; matrix products, arithmetic and copies ran while one was open for 0% of the time, Pallas kernels for 7%

profile of v1, /device:TPU:1, one launch (start us, length us, event | category | flops | bytes accessed | tf_op | source)
XLA Modules:
  0.0 236.4 jit_solution(1787189595819387321)
XLA Ops:
  7.2 0.0 all-reduce.3.cloned.1.call-start
  7.2 0.8 copy.13
  8.0 0.1 reshape.30.colref_ref
  8.1 0.8 copy.12
  8.8 0.0 copy-start.4
  8.9 1.2 copy-done.4
  10.1 0.0 copy-start.3
  10.1 0.0 copy-start.5
  10.1 0.0 copy-start.6
  10.1 61.6 %forward.1 = (bf16[4,8,128,128]{3,2,1,0:T(8,128)(2,1)S(1)}, bf16[4,8,128,128]{3,2,1,0:T(8,128)(2,1)S(1)}, s32[32,1,128]{2,1,0:T(1,128)S(1)}) custom-call(s32[32,1,128]{2,1,0:T(1,128)S(1)} %pad.4.fetch_ref, s32[512]{0:T(512)S(1)} %reshape.30.colref_ref, bf16[32,128,128]{2,1,0:T(8,128)(2,1)S(1)} %bitcast.12, bf16[32,16,128,128]{3,2,1,0:T(8,128)(2,1)} %adj_ref.1), custom_call_target="tpu_custom_call" | custom-call | tf_op jit(solution)/shard_map/forward/pallas_call | solution.py:147
  71.7 0.0 copy-done.3
  71.7 0.0 copy-done.5
  71.7 0.0 copy-done.6
  71.7 8.2 %dense.1 = (bf16[1024,512]{1,0:T(8,128)(2,1)}, bf16[4,2,8,128,128]{4,3,2,1,0:T(8,128)(2,1)}, f32[1024,512]{1,0:T(8,128)}) custom-call(bf16[4,8,128,128]{3,2,1,0:T(8,128)(2,1)S(1)} %get-tuple-element.12.frows_ref, bf16[4,8,128,128]{3,2,1,0:T(8,128)(2,1)S(1)} %get-tuple-element.13.arows_ref, bf16[512,512]{1,0:T(8,128)(2,1)S(1)} %copy-done.5, ...), custom_call_target="tpu_custom_call" | custom-call | tf_op jit(solution)/shard_map/dense/pallas_call | solution.py:216
  79.9 1.7 convert_element_type.6
  81.7 0.0 copy-start.7
  81.7 22.9 %all_to_all.15 = bf16[32,32,512]{2,1,0:T(8,128)(2,1)S(1)} all-to-all(bf16[32,32,512]{2,1,0:T(8,128)(2,1)S(1)} %bitcast.13), channel_id=1, replica_groups=mesh['rows'=32,'cols'=4] {'rows'}, dimensions={0} | all-to-all | bytes 2097152 | tf_op jit(solution)/shard_map/all_to_all | solution.py:340
  104.6 0.8 convert_reduce_fusion
  105.4 0.0 all-reduce.3.cloned.1.call-update
  105.4 0.0 all-gather.2.cloned.1.call-start
  105.5 35.2 %all-reduce.3.cloned.1.call-done = f32[32,512]{1,0:T(8,128)} async-done(((f32[32,512]{1,0:T(8,128)}), f32[32,512]{1,0:T(8,128)}) %all-reduce.3.cloned.1.call-update) | async-done | bytes 65552 | tf_op jit(solution)/shard_map/psum | solution.py:343
  140.7 0.0 all-gather.2.cloned.1.call-update
  140.7 0.0 copy-done.7
  140.7 26.5 %all_to_all.16 = bf16[4,2,8,128,128]{4,3,2,1,0:T(8,128)(2,1)S(1)} all-to-all(bf16[4,2,8,128,128]{4,3,2,1,0:T(8,128)(2,1)S(1)} %copy-done.7), channel_id=1, replica_groups=mesh['rows'=32,'cols'=4] {'cols'}, dimensions={0} | all-to-all | bytes 4194304 | tf_op jit(solution)/shard_map/all_to_all | solution.py:335
  167.3 0.2 fusion
  167.5 13.6 %spread.1 = (bf16[32,128,128]{2,1,0:T(8,128)(2,1)S(1)}, bf16[64,128,128]{2,1,0:T(8,128)(2,1)S(1)}) custom-call(s32[512]{0:T(512)S(1)} %reshape.30.colref_ref, bf16[32,16,128,128]{3,2,1,0:T(8,128)(2,1)} %adj_ref.1, bf16[32,128,128]{2,1,0:T(8,128)(2,1)S(1)} %bitcast.10), custom_call_target="tpu_custom_call" | custom-call | tf_op jit(solution)/shard_map/spread/pallas_call | solution.py:273
  181.1 0.0 copy-start
  181.1 1.3 copy-done
  182.4 0.0 copy-start.1
  182.4 1.0 copy-done.1
  183.4 10.9 %all-to-all-start.2 = ((bf16[32,2,128,128]{3,2,1,0:T(8,128)(2,1)}), bf16[32,2,128,128]{3,2,1,0:T(8,128)(2,1)S(1)}, u32[]{:S(2)}, u32[]{:S(2)}) async-start(bf16[32,2,128,128]{3,2,1,0:T(8,128)(2,1)} %bitcast.11), calls=%async_computation.2 | async-start | bytes 4194304 | tf_op jit(solution)/shard_map/all_to_all | solution.py:339
  194.4 0.1 reshape_squeeze.9.wanted_ref
  194.5 27.7 %all-to-all-done.2 = bf16[32,2,128,128]{3,2,1,0:T(8,128)(2,1)S(1)} async-done(((bf16[32,2,128,128]{3,2,1,0:T(8,128)(2,1)}), bf16[32,2,128,128]{3,2,1,0:T(8,128)(2,1)S(1)}, u32[]{:S(2)}, u32[]{:S(2)}) %all-to-all-start.2) | async-done | bytes 2097184 | tf_op jit(solution)/shard_map/all_to_all | solution.py:339
  222.2 0.0 copy-start.2
  222.2 1.2 copy-done.2
  223.4 3.2 %combine.1 = f32[32,128,128]{2,1,0:T(8,128)} custom-call(s32[64]{0:T(128)S(1)} %reshape_squeeze.9.wanted_ref, bf16[32,128,128]{2,1,0:T(8,128)(2,1)S(1)} %bitcast.9, bf16[32,128,128]{2,1,0:T(8,128)(2,1)S(1)} %copy-done.2, bf16[64,128,128]{2,1,0:T(8,128)(2,1)S(1)} %bitcast.8), custom_call_target="tpu_custom_call" | custom-call | tf_op jit(solution)/shard_map/combine/pallas_call | solution.py:312
  226.6 0.0 all-gather.2.cloned.1.call-done
  226.6 3.0 %fusion.1 = (f32[512,512]{1,0:T(8,128)}, f32[512,512]{1,0:T(8,128)}) fusion(f32[1024,512]{1,0:T(8,128)} %all-gather.2.cloned.1.call-done), kind=kLoop, calls=%fused_computation.3 | loop fusion | bytes 4194304 | tf_op jit(solution)/shard_map/slice | solution.py:346
  (2 shorter events, 0.1 us)
Async XLA Ops:
  7.2 133.5 %all-reduce.3.cloned.1.call-start = ((), (), s32[]{:S(2)}) async-start(), calls=%async_computation.3 | async-start | bytes 131072 | tf_op jit(solution)/shard_map/psum | solution.py:343
  8.8 1.2 copy-start.4
  10.1 61.6 %copy-start.3 = (bf16[1024,512]{1,0:T(8,128)(2,1)S(1)}, bf16[1024,512]{1,0:T(8,128)(2,1)}, u32[]{:S(2)}) copy-start(bf16[1024,512]{1,0:T(8,128)(2,1)} %gout_ref.1) | copy-start | bytes 3145732
  10.1 61.6 %copy-start.5 = (bf16[512,512]{1,0:T(8,128)(2,1)S(1)}, bf16[512,512]{1,0:T(8,128)(2,1)}, u32[]{:S(2)}) copy-start(bf16[512,512]{1,0:T(8,128)(2,1)} %wself_ref.1) | copy-start | bytes 1572868
  10.1 61.6 %copy-start.6 = (bf16[512,512]{1,0:T(8,128)(2,1)S(1)}, bf16[512,512]{1,0:T(8,128)(2,1)}, u32[]{:S(2)}) copy-start(bf16[512,512]{1,0:T(8,128)(2,1)} %wneigh_ref.1) | copy-start | bytes 1572868
  81.7 59.1 %copy-start.7 = (bf16[4,2,8,128,128]{4,3,2,1,0:T(8,128)(2,1)S(1)}, bf16[4,2,8,128,128]{4,3,2,1,0:T(8,128)(2,1)}, u32[]{:S(2)}) copy-start(bf16[4,2,8,128,128]{4,3,2,1,0:T(8,128)(2,1)} %get-tuple-element.17) | copy-start | bytes 6291460
  105.4 121.1 %all-gather.2.cloned.1.call-start = ((), (), s32[]{:S(2)}) async-start(), calls=%async_computation.4 | async-start | bytes 2162688 | tf_op jit(solution)/shard_map/all_gather | solution.py:344
  181.1 1.3 copy-start
  182.4 1.0 copy-start.1
  183.4 38.8 %all-to-all-start.2 = ((bf16[32,2,128,128]{3,2,1,0:T(8,128)(2,1)}), bf16[32,2,128,128]{3,2,1,0:T(8,128)(2,1)S(1)}, u32[]{:S(2)}, u32[]{:S(2)}) async-start(bf16[32,2,128,128]{3,2,1,0:T(8,128)(2,1)} %bitcast.11), calls=%async_computation.2 | async-start | bytes 4194304 | tf_op jit(solution)/shard_map/all_to_all | solution.py:339
  222.2 1.2 copy-start.2
Sparse Core Ops, SparseCore 0:
  105.5 35.1 all-reduce.2
  143.2 46.3 all-gather.1

commit v2 on v1

v2 whole, which is shorter than its diff:
```python
import functools
import math

import jax
import jax.numpy as jnp
from jax import lax
from jax.experimental import pallas as pl
from jax.experimental.pallas import tpu as pltpu
from jax.sharding import PartitionSpec as P

MESH = pl.DeviceIdType.MESH
ANY = pl.BlockSpec(memory_space=pl.ANY)
VMEM = pl.BlockSpec(memory_space=pltpu.VMEM)
SMEM = pl.BlockSpec(memory_space=pltpu.SMEM)
BF16 = jnp.bfloat16
F32 = jnp.float32


def remote(src, dst, send, recv, axis, peer):
    return pltpu.make_async_remote_copy(
        src_ref=src, dst_ref=dst, send_sem=send, recv_sem=recv,
        device_id={axis: peer}, device_id_type=MESH,
    )


def layer_kernel(parts, cols, cap, blocks, per_block, step, fetch_ref, colref_ref, feats_hbm, adj_hbm, w_self_hbm,
                 w_neigh_hbm, gout_hbm, act_ref, self_ref, gagg_hbm, w_ref, wanted_ref,
                 pool, own_v, adj_v, stage, agg_v, frows, arows, w_v, gout_v, gagg_v, gw, idx_v, idx_s,
                 pool_sem, adj_sem, own_sem, ownv_sem, w_sem, gout_sem, smem_sem,
                 idx_send, idx_recv, tile_send, tile_recv, f_send, f_recv, a_send, a_recv, g_send, g_recv):
    me = lax.axis_index("rows")
    mc = lax.axis_index("cols")
    share = blocks // cols
    groups = share // step
    tile, width = own_v.shape[1:]
    hid = cols * width

    local = [
        pltpu.make_async_copy(feats_hbm, own_v, ownv_sem),
        pltpu.make_async_copy(feats_hbm, pool.at[pl.ds(0, blocks)], pool_sem),
        pltpu.make_async_copy(feats_hbm.at[pl.ds(mc * share, share)], frows.at[mc], own_sem),
        pltpu.make_async_copy(w_self_hbm, w_v.at[pl.ds(0, hid)], w_sem.at[0]),
        pltpu.make_async_copy(w_neigh_hbm, w_v.at[pl.ds(hid, hid)], w_sem.at[1]),
        pltpu.make_async_copy(gout_hbm, gout_v, gout_sem),
    ]
    for q in range(cols):
        part = pl.ds(q * share, share)
        local.append(pltpu.make_async_copy(adj_hbm.at[part], adj_v.at[part], adj_sem.at[q]))
    local[0].start()

    barrier = pltpu.get_barrier_semaphore()

    def hello(d, _):
        pl.semaphore_signal(barrier, inc=1, device_id={"rows": lax.rem(me + d, parts)}, device_id_type=MESH)
        return 0

    lax.fori_loop(1, parts, hello, 0)
    for d in range(1, cols):
        pl.semaphore_signal(barrier, inc=1, device_id={"cols": lax.rem(mc + d, cols)}, device_id_type=MESH)
    pl.semaphore_wait(barrier, parts - 1 + cols - 1)

    def ask(d, _):
        p = lax.rem(me + d, parts)
        remote(fetch_ref.at[p], idx_v.at[me], idx_send.at[p], idx_recv.at[me], "rows", p).start()
        return 0

    lax.fori_loop(1, parts, ask, 0)
    idx_v[me] = jnp.full(idx_v.shape[1:], -1, jnp.int32)
    local[0].wait()

    def asked(d, _):
        p = lax.rem(me + parts - d, parts)
        remote(fetch_ref.at[p], idx_v.at[p], idx_send.at[p], idx_recv.at[p], "rows", p).wait_recv()
        return 0

    lax.fori_loop(1, parts, asked, 0)
    to_smem = pltpu.make_async_copy(idx_v, idx_s, smem_sem)
    to_smem.start()
    to_smem.wait()
    wanted_ref[...] = idx_v[...]

    def give(d, _):
        p = lax.rem(me + d, parts)
        for s in range(cap):
            stage[p, s] = own_v[jnp.maximum(idx_s[p, 0, s], 0)]
        remote(stage.at[p], pool.at[pl.ds(blocks + me * cap, cap)], tile_send.at[p], tile_recv.at[me], "rows", p).start()
        return 0

    lax.fori_loop(1, parts, give, 0)

    for d in range(1, cols):
        p = lax.rem(mc + d, cols)
        remote(own_v.at[pl.ds(p * share, share)], frows.at[mc], f_send.at[p], f_recv.at[mc], "cols", p).start()
    for copy in local[1:]:
        copy.start()
    pool[pl.ds(blocks + me * cap, cap)] = jnp.zeros((cap,) + pool.shape[1:], BF16)
    for copy in local[1:]:
        copy.wait()
    for d in range(1, cols):
        p = lax.rem(mc + d, cols)
        remote(own_v.at[pl.ds(p * share, share)], frows.at[p], f_send.at[p], f_recv.at[p], "cols", p).wait()

    def given(d, _):
        p = lax.rem(me + parts - d, parts)
        remote(stage.at[p], pool.at[pl.ds(blocks + p * cap, cap)], tile_send.at[p], tile_recv.at[p], "rows", p).wait_recv()
        return 0

    lax.fori_loop(1, parts, given, 0)

    def aggregate(b):
        left = jnp.concatenate([adj_v[b, k] for k in range(per_block)], axis=1)
        right = jnp.concatenate([pool[colref_ref[b * per_block + k]] for k in range(per_block)], axis=0)
        return jnp.dot(left, right, preferred_element_type=F32).astype(BF16)

    def agg_copy(p, slot, i):
        return remote(agg_v.at[p, i], arows.at[slot, i], a_send.at[p, i], a_recv.at[slot, i], "cols", p)

    def back_copy(p, slot, g):
        part = pl.ds(g * step, step)
        return remote(gagg_v.at[p, part], gagg_hbm.at[slot, part], g_send.at[p, g], g_recv.at[slot, g], "cols", p)

    def tile_round(i):
        def one(d, _):
            p = lax.rem(mc + d, cols)
            agg_v[p, i] = aggregate(p * share + i)
            agg_copy(p, mc, i).start()
            return 0

        lax.fori_loop(1, cols, one, 0)
        arows[mc, i] = aggregate(mc * share + i)

    def dense(g):
        part = pl.ds(g * step, step)
        for j in range(step):
            for d in range(1, cols):
                p = lax.rem(mc + d, cols)
                agg_copy(p, p, g * step + j).wait_recv()

        def rows_of(ref):
            return jnp.concatenate([ref[c, part].reshape(step * tile, width) for c in range(cols)], axis=1)

        both = jnp.concatenate([rows_of(frows), rows_of(arows)], axis=1)
        v = jnp.dot(both, w_v[...], preferred_element_type=F32)
        c0 = math.sqrt(2.0 / math.pi)
        v2 = v * v
        t = jnp.tanh(c0 * v * (1.0 + 0.044715 * v2))
        half = 0.5 * (1.0 + t)
        act_ref[part] = (v * half).astype(BF16).reshape(step, tile, hid)
        slope = half + (0.5 * v) * (1.0 - t * t) * (c0 * (1.0 + 3.0 * 0.044715 * v2))
        grad_pre = (gout_v[part].reshape(step * tile, hid).astype(F32) * slope).astype(BF16)
        nt = (((1,), (1,)), ((), ()))
        out = lax.dot_general(grad_pre, w_v[pl.ds(hid, hid)], nt, preferred_element_type=F32).astype(BF16)
        for c in range(cols):
            gagg_v[c, part] = out[:, c * width:(c + 1) * width].reshape(step, tile, width)
        for d in range(1, cols):
            back_copy(lax.rem(mc + d, cols), mc, g).start()
        out = lax.dot_general(grad_pre, w_v[pl.ds(0, hid)], nt, preferred_element_type=F32).astype(BF16)
        for c in range(cols):
            self_ref[c, part] = out[:, c * width:(c + 1) * width].reshape(step, tile, width)
        gw[...] += lax.dot_general(both, grad_pre, (((0,), (0,)), ((), ())), preferred_element_type=F32)

    gw[...] = jnp.zeros_like(gw)

    def work(g, _):
        @pl.when(g < groups)
        def _():
            for j in range(step):
                tile_round(g * step + j)

        @pl.when(g > 0)
        def _():
            dense(g - 1)

        return 0

    lax.fori_loop(0, groups + 1, work, 0)
    own_back = pltpu.make_async_copy(gagg_v.at[mc], gagg_hbm.at[mc], own_sem)
    own_back.start()

    halves, _, chips, rows_p, cols_p = w_ref.shape
    wide = hid // cols_p
    for n in range(halves * cols):
        for q in range(chips):
            at = n * (2 * hid // (halves * cols)) + (q // wide) * rows_p
            w_ref[n // cols, n % cols, q] = gw[at:at + rows_p, (q % wide) * cols_p:(q % wide + 1) * cols_p]

    own_back.wait()

    def drain(d, _):
        p = lax.rem(me + d, parts)
        remote(fetch_ref.at[p], idx_v.at[p], idx_send.at[p], idx_recv.at[p], "rows", p).wait_send()
        remote(stage.at[p], pool.at[pl.ds(blocks + p * cap, cap)], tile_send.at[p], tile_recv.at[p], "rows", p).wait_send()
        return 0

    lax.fori_loop(1, parts, drain, 0)

    def drain_agg(i, _):
        for d in range(1, cols):
            p = lax.rem(mc + d, cols)
            agg_copy(p, p, i).wait_send()
        return 0

    lax.fori_loop(0, share, drain_agg, 0)

    def drain_back(g, _):
        for d in range(1, cols):
            p = lax.rem(mc + d, cols)
            back_copy(p, p, g).wait()
        return 0

    lax.fori_loop(0, groups, drain_back, 0)


def layer(fetch, colref, feats, adj, w_self, w_neigh, gout, parts, cols, cap):
    blocks, per_block, tile, _ = adj.shape
    width = feats.shape[-1]
    share = blocks // cols
    hid = cols * width
    step = 2
    chips = parts // 2
    piece = (16, 2 * hid * hid // (2 * cols * chips * 16))
    DMA = pltpu.SemaphoreType.DMA
    rows_shape = (cols, share, tile, width)
    return pl.pallas_call(
        functools.partial(layer_kernel, parts, cols, cap, blocks, per_block, step),
        out_shape=(
            jax.ShapeDtypeStruct(gout.shape, BF16),
            jax.ShapeDtypeStruct(rows_shape, BF16),
            jax.ShapeDtypeStruct(rows_shape, BF16),
            jax.ShapeDtypeStruct((2, cols, chips) + piece, F32),
            jax.ShapeDtypeStruct(fetch.shape, jnp.int32),
        ),
        in_specs=[VMEM, SMEM, ANY, ANY, ANY, ANY, ANY],
        out_specs=(VMEM, VMEM, ANY, VMEM, VMEM),
        scratch_shapes=[
            pltpu.VMEM((blocks + parts * cap, tile, width), BF16),
            pltpu.VMEM(feats.shape, BF16),
            pltpu.VMEM(adj.shape, BF16),
            pltpu.VMEM((parts, cap, tile, width), BF16),
            pltpu.VMEM(rows_shape, BF16),
            pltpu.VMEM(rows_shape, BF16),
            pltpu.VMEM(rows_shape, BF16),
            pltpu.VMEM((2 * hid, hid), BF16),
            pltpu.VMEM(gout.shape, BF16),
            pltpu.VMEM(rows_shape, BF16),
            pltpu.VMEM((2 * hid, hid), F32),
            pltpu.VMEM(fetch.shape, jnp.int32),
            pltpu.SMEM(fetch.shape, jnp.int32),
            DMA, DMA((cols,)), DMA, DMA, DMA((2,)), DMA, DMA,
            DMA((parts,)), DMA((parts,)), DMA((parts,)), DMA((parts,)),
            DMA((cols,)), DMA((cols,)), DMA((cols, share)), DMA((cols, share)),
            DMA((cols, share // step)), DMA((cols, share // step)),
        ],
        compiler_params=pltpu.CompilerParams(collective_id=0, has_side_effects=True, vmem_limit_bytes=52 << 20),
        name="layer",
    )(fetch, colref, feats, adj, w_self, w_neigh, gout)


def spread_kernel(per_step, colref_ref, adj_ref, gagg_ref, own_ref, share_ref, pool):
    step_id = pl.program_id(0)
    blocks = own_ref.shape[0]
    per_block = adj_ref.shape[1]
    width = pool.shape[1]

    @pl.when(step_id == 0)
    def _():
        pool[...] = jnp.zeros_like(pool)

    for j in range(per_step):
        b = step_id * per_step + j
        grad_t = gagg_ref[j].T
        for k in range(0, per_block, 2):
            pair = jnp.concatenate([adj_ref[j, k], adj_ref[j, k + 1]], axis=1)
            out = jnp.dot(grad_t, pair, preferred_element_type=F32)
            half = out.shape[1] // 2
            pool[colref_ref[b * per_block + k]] += out[:, :half]
            pool[colref_ref[b * per_block + k + 1]] += out[:, half:]

    @pl.when(step_id == pl.num_programs(0) - 1)
    def _():
        def own(t, _):
            own_ref[t] = pool[t].astype(BF16).T
            return 0

        def away(t, _):
            share_ref[t] = pool[blocks + t].astype(BF16).T
            return 0

        lax.fori_loop(0, blocks, own, 0, unroll=4)
        lax.fori_loop(0, share_ref.shape[0], away, 0, unroll=4)


def spread(colref, adj, gagg, slots):
    blocks, per_block, tile, _ = adj.shape
    width = gagg.shape[-1]
    per_step = 4
    return pl.pallas_call(
        functools.partial(spread_kernel, per_step),
        grid=(blocks // per_step,),
        out_shape=(
            jax.ShapeDtypeStruct((blocks, tile, width), BF16),
            jax.ShapeDtypeStruct((slots, tile, width), BF16),
        ),
        in_specs=[
            SMEM,
            pl.BlockSpec((per_step, per_block, tile, tile), lambda i: (i, 0, 0, 0)),
            pl.BlockSpec((per_step, tile, width), lambda i: (i, 0, 0)),
        ],
        out_specs=(
            pl.BlockSpec((blocks, tile, width), lambda i: (0, 0, 0)),
            pl.BlockSpec((slots, tile, width), lambda i: (0, 0, 0)),
        ),
        scratch_shapes=[pltpu.VMEM((blocks + slots, width, tile), F32)],
        compiler_params=pltpu.CompilerParams(vmem_limit_bytes=48 << 20),
        name="spread",
    )(colref, adj, gagg)


def finish_kernel(parts, cols, share_hbm, self_hbm, w_ref, ret_hbm, selfp_hbm, sums_ref,
                  from_core, to_z, from_z, to_chip, from_chip, sums,
                  s_send, s_recv, p_send, p_recv, own_sem,
                  core_send, core_recv, z_send, z_recv, chip_send, chip_recv, up_send, up_recv):
    me = lax.axis_index("rows")
    mc = lax.axis_index("cols")
    core = lax.rem(me, 2)
    chip = me // 2
    chips = parts // 2
    mate = me + 1 - 2 * core

    barrier = pltpu.get_barrier_semaphore()

    def hello(d, _):
        pl.semaphore_signal(barrier, inc=1, device_id={"rows": lax.rem(me + d, parts)}, device_id_type=MESH)
        return 0

    lax.fori_loop(1, parts, hello, 0)
    for d in range(1, cols):
        pl.semaphore_signal(barrier, inc=1, device_id={"cols": lax.rem(mc + d, cols)}, device_id_type=MESH)
    pl.semaphore_wait(barrier, parts - 1 + cols - 1)

    def share_copy(p, slot):
        return remote(share_hbm.at[p], ret_hbm.at[slot], s_send.at[p], s_recv.at[slot], "rows", p)

    def shares(lo, hi):
        def one(d, _):
            share_copy(lax.rem(me + d, parts), me).start()
            return 0

        lax.fori_loop(lo, hi, one, 0)

    def self_copy(p, slot):
        return remote(self_hbm.at[p], selfp_hbm.at[slot], p_send.at[p], p_recv.at[slot], "cols", p)

    def others():
        return [lax.rem(mc + d, cols) for d in range(1, cols)]

    def over_chips(f):
        def one(d, _):
            f(lax.rem(chip + d, chips))
            return 0

        lax.fori_loop(1, chips, one, 0)

    pair = remote(w_ref.at[1 - core], from_core, core_send.at[0], core_recv.at[0], "rows", mate)
    pair.start()
    third = parts // 3
    shares(1, third)
    pair.wait()
    for c in range(cols):
        from_core[c] = from_core[c] + w_ref[core, c]
        to_z[c] = from_core[c].astype(BF16)

    def z_copy(p, slot):
        return remote(to_z.at[p], from_z.at[slot], z_send.at[0, p], z_recv.at[0, slot], "cols", p)

    for p in others():
        z_copy(p, mc).start()
    shares(third, 2 * third)
    for p in others():
        z_copy(p, p).wait()
    total = from_core[mc]
    for p in others():
        total = total + from_z[p].astype(F32)
    to_chip[...] = total.astype(BF16)

    def chip_copy(q, slot):
        return remote(to_chip.at[q], from_chip.at[slot], chip_send.at[q], chip_recv.at[slot], "rows", 2 * q + core)

    over_chips(lambda q: chip_copy(q, chip).start())
    shares(2 * third, parts)
    for p in others():
        self_copy(p, mc).start()
    own = pltpu.make_async_copy(self_hbm.at[mc], selfp_hbm.at[mc], own_sem)
    own.start()
    from_chip[chip] = to_chip[chip]
    over_chips(lambda q: chip_copy(q, q).wait())
    total = from_chip[0].astype(F32)
    for q in range(1, chips):
        total = total + from_chip[q].astype(F32)
    sums[core, mc, chip] = total.astype(BF16)

    def up_copy(q, slot):
        return remote(sums.at[core, mc, chip], sums.at[core, mc, slot], up_send.at[q], up_recv.at[slot], "rows", 2 * q + core)

    over_chips(lambda q: up_copy(q, chip).start())
    over_chips(lambda q: up_copy(q, q).wait())

    def z_up(p, slot):
        return remote(sums.at[core, mc], sums.at[core, slot], z_send.at[1, p], z_recv.at[1, slot], "cols", p)

    for p in others():
        z_up(p, mc).start()
    for p in others():
        z_up(p, p).wait()
    pair_up = remote(sums.at[core], sums.at[core], core_send.at[1], core_recv.at[1], "rows", mate)
    pair_up.start()
    pair_up.wait()
    sums_ref[...] = sums[...]

    for p in others():
        self_copy(p, p).wait()
    own.wait()

    def drain(d, _):
        p = lax.rem(me + d, parts)
        share_copy(p, p).wait()
        return 0

    lax.fori_loop(1, parts, drain, 0)


def finish(shares, self_rows, w):
    parts, cap, tile, width = shares.shape
    cols = self_rows.shape[0]
    chips = w.shape[2]
    piece = w.shape[3:]
    DMA = pltpu.SemaphoreType.DMA
    return pl.pallas_call(
        functools.partial(finish_kernel, parts, cols),
        out_shape=(
            jax.ShapeDtypeStruct(shares.shape, BF16),
            jax.ShapeDtypeStruct(self_rows.shape, BF16),
            jax.ShapeDtypeStruct(w.shape, BF16),
        ),
        in_specs=[ANY, ANY, VMEM],
        out_specs=(ANY, ANY, VMEM),
        scratch_shapes=[
            pltpu.VMEM((cols, chips) + piece, F32),
            pltpu.VMEM((cols, chips) + piece, BF16),
            pltpu.VMEM((cols, chips) + piece, BF16),
            pltpu.VMEM((chips,) + piece, BF16),
            pltpu.VMEM((chips,) + piece, BF16),
            pltpu.VMEM(w.shape, BF16),
            DMA((parts,)), DMA((parts,)), DMA((cols,)), DMA((cols,)), DMA,
            DMA((2,)), DMA((2,)), DMA((2, cols)), DMA((2, cols)),
            DMA((chips,)), DMA((chips,)), DMA((chips,)), DMA((chips,)),
        ],
        compiler_params=pltpu.CompilerParams(collective_id=1, has_side_effects=True, vmem_limit_bytes=40 << 20),
        name="finish",
    )(shares, self_rows, w)


def combine_kernel(scale, wanted_ref, self_ref, own_ref, back_ref, sums_ref, out_ref, gs_ref, gn_ref):
    slots = back_ref.shape[0]
    out_ref[...] = self_ref[...].astype(F32) + own_ref[...].astype(F32)

    def add(s, _):
        t = wanted_ref[s]

        @pl.when(t >= 0)
        def _():
            out_ref[t] += back_ref[s].astype(F32)

        return 0

    lax.fori_loop(0, slots, add, 0)
    halves, cols, chips, rows_p, cols_p = sums_ref.shape
    hid = gs_ref.shape[0]
    wide = hid // cols_p
    for half, ref in enumerate((gs_ref, gn_ref)):
        for c in range(cols):
            for q in range(chips):
                at = c * (hid // cols) + (q // wide) * rows_p
                ref[at:at + rows_p, (q % wide) * cols_p:(q % wide + 1) * cols_p] = sums_ref[half, c, q].astype(F32) * scale


def combine(wanted, self_part, own, back, sums, scale):
    hid = own.shape[-1] * sums.shape[1]
    weights = jax.ShapeDtypeStruct((hid, hid), F32)
    return pl.pallas_call(
        functools.partial(combine_kernel, scale),
        out_shape=(jax.ShapeDtypeStruct(own.shape, F32), weights, weights),
        in_specs=[SMEM, VMEM, VMEM, VMEM, VMEM],
        out_specs=(VMEM, VMEM, VMEM),
        compiler_params=pltpu.CompilerParams(vmem_limit_bytes=40 << 20),
        name="combine",
    )(wanted, self_part, own, back, sums)


def body(feats, adj_vals, colref, fetch_ids, w_self, w_neigh, grad_out):
    node_rows, width = feats.shape
    blocks, per_block, tile, _ = adj_vals.shape
    parts = lax.axis_size("rows")
    cols = lax.axis_size("cols")
    cap = fetch_ids.shape[2]
    slots = parts * cap
    hid = width * cols
    scale = 1.0 / math.sqrt(node_rows * parts)
    fetch = jnp.pad(fetch_ids.reshape(parts, 1, cap), ((0, 0), (0, 0), (0, 128 - cap)))
    refs = colref.reshape(blocks * per_block)
    gout = grad_out.reshape(blocks // cols, tile, hid)
    act, self_rows, gagg, w, wanted = layer(
        fetch, refs, feats.reshape(blocks, tile, width), adj_vals, w_self, w_neigh, gout, parts, cols, cap
    )
    own, shares = spread(refs, adj_vals, gagg.reshape(blocks, tile, width), slots)
    returned, self_part, sums = finish(shares.reshape(parts, cap, tile, width), self_rows, w)
    grad_feats, grad_self, grad_neigh = combine(
        wanted[:, 0, :cap].reshape(slots), self_part.reshape(blocks, tile, width), own,
        returned.reshape(slots, tile, width), sums, scale,
    )
    return act.reshape(grad_out.shape), grad_self, grad_neigh, grad_feats.reshape(node_rows, width)


def solution(mesh):
    in_specs = (
        P("rows", "cols"),
        P("rows", None, None, None),
        P("rows", None),
        P("rows", None, None),
        P(),
        P(),
        P(("rows", "cols"), None),
    )
    out_specs = (P(("rows", "cols"), None), P(), P(), P("rows", "cols"))
    return jax.shard_map(body, mesh=mesh, in_specs=in_specs, out_specs=out_specs, check_vma=False)
```

time: 238 us -> 153 us (0.64)
  waiting for transfers between devices: 63 us -> 0 us
  Pallas kernels: 86.6 us -> 146 us
  blocking collectives: 49.5 us -> 0 us
  between operations: 14.1 us -> 0.71 us
  starting transfers between devices: 11 us -> 0 us
  local copies, waits for them, and re-layouts: 9.73 us -> 6.05 us
  other arithmetic: 2.51 us -> 0 us
    pallas_call x3, Pallas kernels: 73 us -> 132 us  [the longest x1 75.4 us: layer(): pl.pallas_call(functools.partial(layer_kernel, parts, cols, cap, blocks,...]
    all_to_all x2 -> x0, blocking collectives: 49.5 us -> none  [the longest x1 26.5 us: body(): back = lax.all_to_all(back, 'cols', split_axis=0, concat_axis=0, tiled=True)]
    psum x1 -> x0, waiting for transfers between devices: 35.2 us -> none  [body(): piece = lax.psum(pieces.astype(F32).sum(axis=0), 'cols')]
    all_to_all x1 -> x0, waiting for transfers between devices: 27.7 us -> none  [body(): lax.all_to_all(shares.reshape(parts, cap, tile, width), 'rows', split_axi...]
    all_to_all x1 -> x0, starting transfers between devices: 10.9 us -> none  [body(): lax.all_to_all(shares.reshape(parts, cap, tile, width), 'rows', split_axi...]
    slice x2 -> x0, local copies, waits for them, and re-layouts: 3.21 us -> none  [the longest x1 3.03 us: body(): return (act, sums[:hid], sums[hid:], grad_feats.reshape(node_rows, width))]
    unnamed x17 -> x14, local copies, waits for them, and re-layouts: 5.52 us -> 5.05 us
  transfers between devices with their start and end apart: 3 -> 0, of which waited for: 2 -> 0; matrix products, arithmetic and copies ran while one was open for 0% -> 0% of each run, Pallas kernels for 7% -> 0%
where the time goes in v2:
time: 153 us
  Pallas kernels  146 us (95%)
  local copies, waits for them, and re-layouts  6.05 us (4%)
    pallas_call x1, Pallas kernels, layer(): pl.pallas_call(functools.partial(layer_kernel, parts, cols, cap, blocks,...  75.4 us
    pallas_call x1, Pallas kernels, finish(): pl.pallas_call(functools.partial(finish_kernel, parts, cols), out_shape=(...  52.7 us
    pallas_call x1, Pallas kernels, spread(): pl.pallas_call(functools.partial(spread_kernel, per_step), grid=(blocks /...  13.7 us
    unnamed x14, local copies, waits for them, and re-layouts  5.05 us
    pallas_call x1, Pallas kernels, combine(): pl.pallas_call(functools.partial(combine_kernel, scale), out_shape=(jax.S...  4.02 us

profile of v2, /device:TPU:1, one launch (start us, length us, event | category | flops | bytes accessed | tf_op | source)
XLA Modules:
  0.0 152.6 jit_solution(1532033076602421348)
XLA Ops:
  0.6 0.8 copy.13
  1.4 0.1 reshape.39.colref_ref
  1.5 0.8 copy.12
  2.3 0.0 copy-start.3
  2.3 1.0 copy-done.3
  3.3 0.0 copy-start.4
  3.3 1.0 copy-done.4
  4.4 75.4 %layer.1 = (bf16[8,128,512]{2,1,0:T(8,128)(2,1)}, bf16[4,8,128,128]{3,2,1,0:T(8,128)(2,1)}, bf16[4,8,128,128]{3,2,1,0:T(8,128)(2,1)}, f32[2,4,16,16,256]{4,3,2,1,0:T(8,128)}, s32[32,1,128]{2,1,0:T(1,128)S(1)}) custom-call(s32[32,1,128]{2,1,0:T(1,128)S(1)} %pad.4.fetch_ref, s32[512]{0:T(512)S(1)} %reshape.39.colref_ref, bf16[32,128,128]{2,1,0:T(8,128)(2,1)} %bitcast.13, ...), custom_call_target="tpu_custom_call" | custom-call | tf_op jit(solution)/shard_map/layer/pallas_call | solution.py:224
  79.8 0.1 reshape_squeeze.3.wanted_ref
  79.9 0.0 copy-start.2
  79.9 1.2 copy-done.2
  81.1 0.0 copy-start
  81.1 0.0 copy-start.1
  81.1 13.7 %spread.1 = (bf16[32,128,128]{2,1,0:T(8,128)(2,1)S(1)}, bf16[64,128,128]{2,1,0:T(8,128)(2,1)S(1)}) custom-call(s32[512]{0:T(512)S(1)} %reshape.39.colref_ref, bf16[32,16,128,128]{3,2,1,0:T(8,128)(2,1)} %adj_ref.1, bf16[32,128,128]{2,1,0:T(8,128)(2,1)S(1)} %bitcast.11), custom_call_target="tpu_custom_call" | custom-call | tf_op jit(solution)/shard_map/spread/pallas_call | solution.py:297
  94.9 0.0 copy-done
  94.9 0.0 copy-done.1
  94.9 52.7 %finish.1 = (bf16[32,2,128,128]{3,2,1,0:T(8,128)(2,1)S(1)}, bf16[4,8,128,128]{3,2,1,0:T(8,128)(2,1)S(1)}, bf16[2,4,16,16,256]{4,3,2,1,0:T(8,128)(2,1)S(1)}) custom-call(bf16[32,2,128,128]{3,2,1,0:T(8,128)(2,1)S(1)} %bitcast.10, bf16[4,8,128,128]{3,2,1,0:T(8,128)(2,1)S(1)} %copy-done.1, f32[2,4,16,16,256]{4,3,2,1,0:T(8,128)S(1)} %copy-done), custom_call_target="tpu_custom_call" | custom-call | tf_op jit(solution)/shard_map/finish/pallas_call | solution.py:438
  147.6 0.0 copy-start.5
  147.6 4.0 %combine.1 = (f32[32,128,128]{2,1,0:T(8,128)}, f32[512,512]{1,0:T(8,128)}, f32[512,512]{1,0:T(8,128)}) custom-call(s32[64]{0:T(128)S(1)} %reshape_squeeze.3.wanted_ref, bf16[32,128,128]{2,1,0:T(8,128)(2,1)S(1)} %bitcast.12, bf16[32,128,128]{2,1,0:T(8,128)(2,1)S(1)} %get-tuple-element.24.own_ref, bf16[64,128,128]{2,1,0:T(8,128)(2,1)S(1)} %bitcast.9, ...), custom_call_target="tpu_custom_call" | custom-call | tf_op jit(solution)/shard_map/combine/pallas_call | solution.py:490
  151.6 0.0 copy-done.5
  151.6 1.0 copy.15
  (2 shorter events, 0.1 us)
Async XLA Ops:
  2.3 1.0 copy-start.3
  3.3 1.0 copy-start.4
  79.9 1.2 copy-start.2
  81.1 13.7 %copy-start = (f32[2,4,16,16,256]{4,3,2,1,0:T(8,128)S(1)}, f32[2,4,16,16,256]{4,3,2,1,0:T(8,128)}, u32[]{:S(2)}) copy-start(f32[2,4,16,16,256]{4,3,2,1,0:T(8,128)} %get-tuple-element.22.w_ref) | copy-start | bytes 6291460
  81.1 13.7 %copy-start.1 = (bf16[4,8,128,128]{3,2,1,0:T(8,128)(2,1)S(1)}, bf16[4,8,128,128]{3,2,1,0:T(8,128)(2,1)}, u32[]{:S(2)}) copy-start(bf16[4,8,128,128]{3,2,1,0:T(8,128)(2,1)} %get-tuple-element.21.self_hbm) | copy-start | bytes 3145732
  147.6 4.0 %copy-start.5 = (bf16[8,128,512]{2,1,0:T(8,128)(2,1)S(1)}, bf16[8,128,512]{2,1,0:T(8,128)(2,1)}, u32[]{:S(2)}) copy-start(bf16[8,128,512]{2,1,0:T(8,128)(2,1)} %get-tuple-element.17) | copy-start | bytes 3145732

commit v3 on v2

--- a/solution.py
+++ b/solution.py
@@ -23,11 +23,27 @@
     )
 
 
+def send_order(parts):
+    side = math.isqrt(parts // 2)
+    hops = lambda n: min(n, side - n)
+    offsets = [(y, x, c) for y in range(side) for x in range(side) for c in range(2)][1:]
+    return sorted(offsets, key=lambda o: (-hops(o[0]) - hops(o[1]), o[2]))
+
+
+def at_offset(me, parts, offset):
+    side = math.isqrt(parts // 2)
+    dy, dx, dc = offset
+    core, chip = lax.rem(me, 2), me // 2
+    y, x = lax.rem(chip // side + dy, side), lax.rem(lax.rem(chip, side) + dx, side)
+    return (y * side + x) * 2 + (1 - core if dc else core)
+
+
 def layer_kernel(parts, cols, cap, blocks, per_block, step, fetch_ref, colref_ref, feats_hbm, adj_hbm, w_self_hbm,
-                 w_neigh_hbm, gout_hbm, act_ref, self_ref, gagg_hbm, w_ref, wanted_ref,
-                 pool, own_v, adj_v, stage, agg_v, frows, arows, w_v, gout_v, gagg_v, gw, idx_v, idx_s,
+                 w_neigh_hbm, gout_hbm, act_ref, self_ref, gagg_hbm, w_own_ref, w_send_refs, wanted_ref,
+                 pool, own_v, adj_v, stage, agg_v, frows, arows, w_v, gout_v, gagg_v, gw, from_core, w_half, idx_v, idx_s,
                  pool_sem, adj_sem, own_sem, ownv_sem, w_sem, gout_sem, smem_sem,
-                 idx_send, idx_recv, tile_send, tile_recv, f_send, f_recv, a_send, a_recv, g_send, g_recv):
+                 idx_send, idx_recv, tile_send, tile_recv, f_send, f_recv, a_send, a_recv, g_send, g_recv,
+                 core_send, core_recv):
     me = lax.axis_index("rows")
     mc = lax.axis_index("cols")
     share = blocks // cols
@@ -61,7 +77,7 @@
 
     def ask(d, _):
         p = lax.rem(me + d, parts)
-        remote(fetch_ref.at[p], idx_v.at[me], idx_send.at[p], idx_recv.at[me], "rows", p).start()
+        remote(fetch_ref, idx_v.at[me], idx_send.at[p], idx_recv.at[me], "rows", p).start()
         return 0
 
     lax.fori_loop(1, parts, ask, 0)
@@ -70,29 +86,31 @@
 
     def asked(d, _):
         p = lax.rem(me + parts - d, parts)
-        remote(fetch_ref.at[p], idx_v.at[p], idx_send.at[p], idx_recv.at[p], "rows", p).wait_recv()
+        remote(fetch_ref, idx_v.at[p], idx_send.at[p], idx_recv.at[p], "rows", p).wait_recv()
         return 0
 
     lax.fori_loop(1, parts, asked, 0)
     to_smem = pltpu.make_async_copy(idx_v, idx_s, smem_sem)
     to_smem.start()
     to_smem.wait()
-    wanted_ref[...] = idx_v[...]
-
-    def give(d, _):
-        p = lax.rem(me + d, parts)
+    for offset in send_order(parts):
+        p = at_offset(me, parts, offset)
         for s in range(cap):
-            stage[p, s] = own_v[jnp.maximum(idx_s[p, 0, s], 0)]
+            stage[p, s] = own_v[jnp.maximum(idx_s[p, s, me], 0)]
         remote(stage.at[p], pool.at[pl.ds(blocks + me * cap, cap)], tile_send.at[p], tile_recv.at[me], "rows", p).start()
-        return 0
-
-    lax.fori_loop(1, parts, give, 0)
 
     for d in range(1, cols):
         p = lax.rem(mc + d, cols)
         remote(own_v.at[pl.ds(p * share, share)], frows.at[mc], f_send.at[p], f_recv.at[mc], "cols", p).start()
     for copy in local[1:]:
         copy.start()
+
+    def want(p, _):
+        for s in range(cap):
+            wanted_ref[p * cap + s] = idx_s[p, s, me]
+        return 0
+
+    lax.fori_loop(0, parts, want, 0)
     pool[pl.ds(blocks + me * cap, cap)] = jnp.zeros((cap,) + pool.shape[1:], BF16)
     for copy in local[1:]:
         copy.wait()
@@ -109,7 +127,7 @@
 
     def aggregate(b):
         left = jnp.concatenate([adj_v[b, k] for k in range(per_block)], axis=1)
-        right = jnp.concatenate([pool[colref_ref[b * per_block + k]] for k in range(per_block)], axis=0)
+        right = jnp.concatenate([pool[colref_ref[k, b]] for k in range(per_block)], axis=0)
         return jnp.dot(left, right, preferred_element_type=F32).astype(BF16)
 
     def agg_copy(p, slot, i):
@@ -157,7 +175,8 @@
         out = lax.dot_general(grad_pre, w_v[pl.ds(0, hid)], nt, preferred_element_type=F32).astype(BF16)
         for c in range(cols):
             self_ref[c, part] = out[:, c * width:(c + 1) * width].reshape(step, tile, width)
-        gw[...] += lax.dot_general(both, grad_pre, (((0,), (0,)), ((), ())), preferred_element_type=F32)
+        sums = lax.dot_general(both, grad_pre, (((0,), (0,)), ((), ())), preferred_element_type=F32)
+        gw[...] += sums.reshape(gw.shape)
 
     gw[...] = jnp.zeros_like(gw)
 
@@ -177,18 +196,27 @@
     own_back = pltpu.make_async_copy(gagg_v.at[mc], gagg_hbm.at[mc], own_sem)
     own_back.start()
 
-    halves, _, chips, rows_p, cols_p = w_ref.shape
+    core = lax.rem(me, 2)
+    mate = me + 1 - 2 * core
+    pair = remote(gw.at[1 - core], from_core, core_send, core_recv, "rows", mate)
+    pair.start()
+    pair.wait()
+    _, chips, rows_p, cols_p = w_half.shape
     wide = hid // cols_p
-    for n in range(halves * cols):
+    for c in range(cols):
         for q in range(chips):
-            at = n * (2 * hid // (halves * cols)) + (q // wide) * rows_p
-            w_ref[n // cols, n % cols, q] = gw[at:at + rows_p, (q % wide) * cols_p:(q % wide + 1) * cols_p]
+            down = pl.ds(c * (hid // cols) + (q // wide) * rows_p, rows_p)
+            across = pl.ds((q % wide) * cols_p, cols_p)
+            w_half[c, q] = gw[core, down, across] + from_core[down, across]
+    w_own_ref[...] = w_half[mc]
+    for d in range(1, cols):
+        w_send_refs[d - 1][...] = w_half[lax.rem(mc + d, cols)].astype(BF16)
 
     own_back.wait()
 
     def drain(d, _):
         p = lax.rem(me + d, parts)
-        remote(fetch_ref.at[p], idx_v.at[p], idx_send.at[p], idx_recv.at[p], "rows", p).wait_send()
+        remote(fetch_ref, idx_v.at[p], idx_send.at[p], idx_recv.at[p], "rows", p).wait_send()
         remote(stage.at[p], pool.at[pl.ds(blocks + p * cap, cap)], tile_send.at[p], tile_recv.at[p], "rows", p).wait_send()
         return 0
 
@@ -227,11 +255,12 @@
             jax.ShapeDtypeStruct(gout.shape, BF16),
             jax.ShapeDtypeStruct(rows_shape, BF16),
             jax.ShapeDtypeStruct(rows_shape, BF16),
-            jax.ShapeDtypeStruct((2, cols, chips) + piece, F32),
-            jax.ShapeDtypeStruct(fetch.shape, jnp.int32),
+            jax.ShapeDtypeStruct((chips,) + piece, F32),
+            (jax.ShapeDtypeStruct((chips,) + piece, BF16),) * (cols - 1),
+            jax.ShapeDtypeStruct((parts * cap,), jnp.int32),
         ),
         in_specs=[VMEM, SMEM, ANY, ANY, ANY, ANY, ANY],
-        out_specs=(VMEM, VMEM, ANY, VMEM, VMEM),
+        out_specs=(VMEM, VMEM, ANY, VMEM, (VMEM,) * (cols - 1), SMEM),
         scratch_shapes=[
             pltpu.VMEM((blocks + parts * cap, tile, width), BF16),
             pltpu.VMEM(feats.shape, BF16),
@@ -243,24 +272,28 @@
             pltpu.VMEM((2 * hid, hid), BF16),
             pltpu.VMEM(gout.shape, BF16),
             pltpu.VMEM(rows_shape, BF16),
-            pltpu.VMEM((2 * hid, hid), F32),
-            pltpu.VMEM(fetch.shape, jnp.int32),
-            pltpu.SMEM(fetch.shape, jnp.int32),
+            pltpu.VMEM((2, hid, hid), F32),
+            pltpu.VMEM((hid, hid), F32),
+            pltpu.VMEM((cols, chips) + piece, F32),
+            pltpu.VMEM((parts,) + fetch.shape, jnp.int32),
+            pltpu.SMEM((parts,) + fetch.shape, jnp.int32),
             DMA, DMA((cols,)), DMA, DMA, DMA((2,)), DMA, DMA,
             DMA((parts,)), DMA((parts,)), DMA((parts,)), DMA((parts,)),
             DMA((cols,)), DMA((cols,)), DMA((cols, share)), DMA((cols, share)),
-            DMA((cols, share // step)), DMA((cols, share // step)),
+            DMA((cols, share // step)), DMA((cols, share // step)), DMA, DMA,
         ],
-        compiler_params=pltpu.CompilerParams(collective_id=0, has_side_effects=True, vmem_limit_bytes=52 << 20),
+        compiler_params=pltpu.CompilerParams(collective_id=0, has_side_effects=True, vmem_limit_bytes=62 << 20),
         name="layer",
     )(fetch, colref, feats, adj, w_self, w_neigh, gout)
 
 
-def spread_kernel(per_step, colref_ref, adj_ref, gagg_ref, own_ref, share_ref, pool):
+def spread_kernel(per_step, colref_ref, adj_ref, gagg_ref, act_ref, own_ref, share_ref, act_out_ref, pool):
     step_id = pl.program_id(0)
     blocks = own_ref.shape[0]
     per_block = adj_ref.shape[1]
     width = pool.shape[1]
+
+    act_out_ref[...] = act_ref[...]
 
     @pl.when(step_id == 0)
     def _():
@@ -273,8 +306,8 @@
             pair = jnp.concatenate([adj_ref[j, k], adj_ref[j, k + 1]], axis=1)
             out = jnp.dot(grad_t, pair, preferred_element_type=F32)
             half = out.shape[1] // 2
-            pool[colref_ref[b * per_block + k]] += out[:, :half]
-            pool[colref_ref[b * per_block + k + 1]] += out[:, half:]
+            pool[colref_ref[k, b]] += out[:, :half]
+            pool[colref_ref[k + 1, b]] += out[:, half:]
 
     @pl.when(step_id == pl.num_programs(0) - 1)
     def _():
@@ -290,7 +323,7 @@
         lax.fori_loop(0, share_ref.shape[0], away, 0, unroll=4)
 
 
-def spread(colref, adj, gagg, slots):
+def spread(colref, adj, gagg, act, slots):
     blocks, per_block, tile, _ = adj.shape
     width = gagg.shape[-1]
     per_step = 4
@@ -300,24 +333,28 @@
         out_shape=(
             jax.ShapeDtypeStruct((blocks, tile, width), BF16),
             jax.ShapeDtypeStruct((slots, tile, width), BF16),
+            jax.ShapeDtypeStruct(act.shape, BF16),
         ),
         in_specs=[
             SMEM,
             pl.BlockSpec((per_step, per_block, tile, tile), lambda i: (i, 0, 0, 0)),
             pl.BlockSpec((per_step, tile, width), lambda i: (i, 0, 0)),
+            pl.BlockSpec((act.shape[0] * per_step // blocks,) + act.shape[1:], lambda i: (i, 0, 0)),
         ],
         out_specs=(
             pl.BlockSpec((blocks, tile, width), lambda i: (0, 0, 0)),
             pl.BlockSpec((slots, tile, width), lambda i: (0, 0, 0)),
+            pl.BlockSpec((act.shape[0] * per_step // blocks,) + act.shape[1:], lambda i: (i, 0, 0)),
         ),
         scratch_shapes=[pltpu.VMEM((blocks + slots, width, tile), F32)],
         compiler_params=pltpu.CompilerParams(vmem_limit_bytes=48 << 20),
+        cost_estimate=pl.CostEstimate(flops=2 * adj.size * width, bytes_accessed=2 * adj.size, transcendentals=0),
         name="spread",
-    )(colref, adj, gagg)
-
-
-def finish_kernel(parts, cols, share_hbm, self_hbm, w_ref, ret_hbm, selfp_hbm, sums_ref,
-                  from_core, to_z, from_z, to_chip, from_chip, sums,
+    )(colref, adj, gagg, act)
+
+
+def finish_kernel(parts, cols, share_hbm, self_hbm, w_own_ref, w_refs, ret_hbm, selfp_hbm, sums_ref,
+                  to_chip, from_chip, sums,
                   s_send, s_recv, p_send, p_recv, own_sem,
                   core_send, core_recv, z_send, z_recv, chip_send, chip_recv, up_send, up_recv):
     me = lax.axis_index("rows")
@@ -341,12 +378,11 @@
     def share_copy(p, slot):
         return remote(share_hbm.at[p], ret_hbm.at[slot], s_send.at[p], s_recv.at[slot], "rows", p)
 
+    order = send_order(parts)
+
     def shares(lo, hi):
-        def one(d, _):
-            share_copy(lax.rem(me + d, parts), me).start()
-            return 0
-
-        lax.fori_loop(lo, hi, one, 0)
+        for offset in order[lo:hi]:
+            share_copy(at_offset(me, parts, offset), me).start()
 
     def self_copy(p, slot):
         return remote(self_hbm.at[p], selfp_hbm.at[slot], p_send.at[p], p_recv.at[slot], "cols", p)
@@ -361,35 +397,18 @@
 
         lax.fori_loop(1, chips, one, 0)
 
-    pair = remote(w_ref.at[1 - core], from_core, core_send.at[0], core_recv.at[0], "rows", mate)
-    pair.start()
-    third = parts // 3
-    shares(1, third)
-    pair.wait()
-    for c in range(cols):
-        from_core[c] = from_core[c] + w_ref[core, c]
-        to_z[c] = from_core[c].astype(BF16)
-
-    def z_copy(p, slot):
-        return remote(to_z.at[p], from_z.at[slot], z_send.at[0, p], z_recv.at[0, slot], "cols", p)
-
-    for p in others():
-        z_copy(p, mc).start()
-    shares(third, 2 * third)
-    for p in others():
-        z_copy(p, p).wait()
-    total = from_core[mc]
-    for p in others():
-        total = total + from_z[p].astype(F32)
+    total = w_own_ref[...]
+    for ref in w_refs:
+        total = total + ref[...].astype(F32)
     to_chip[...] = total.astype(BF16)
 
     def chip_copy(q, slot):
         return remote(to_chip.at[q], from_chip.at[slot], chip_send.at[q], chip_recv.at[slot], "rows", 2 * q + core)
 
     over_chips(lambda q: chip_copy(q, chip).start())
-    shares(2 * third, parts)
     for p in others():
         self_copy(p, mc).start()
+    shares(0, 8)
     own = pltpu.make_async_copy(self_hbm.at[mc], selfp_hbm.at[mc], own_sem)
     own.start()
     from_chip[chip] = to_chip[chip]
@@ -403,16 +422,18 @@
         return remote(sums.at[core, mc, chip], sums.at[core, mc, slot], up_send.at[q], up_recv.at[slot], "rows", 2 * q + core)
 
     over_chips(lambda q: up_copy(q, chip).start())
+    shares(8, 18)
     over_chips(lambda q: up_copy(q, q).wait())
 
     def z_up(p, slot):
-        return remote(sums.at[core, mc], sums.at[core, slot], z_send.at[1, p], z_recv.at[1, slot], "cols", p)
+        return remote(sums.at[core, mc], sums.at[core, slot], z_send.at[p], z_recv.at[slot], "cols", p)
 
     for p in others():
         z_up(p, mc).start()
+    shares(18, parts)
     for p in others():
         z_up(p, p).wait()
-    pair_up = remote(sums.at[core], sums.at[core], core_send.at[1], core_recv.at[1], "rows", mate)
+    pair_up = remote(sums.at[core], sums.at[core], core_send, core_recv, "rows", mate)
     pair_up.start()
     pair_up.wait()
     sums_ref[...] = sums[...]
@@ -429,35 +450,32 @@
     lax.fori_loop(1, parts, drain, 0)
 
 
-def finish(shares, self_rows, w):
+def finish(shares, self_rows, w_own, w_in):
     parts, cap, tile, width = shares.shape
     cols = self_rows.shape[0]
-    chips = w.shape[2]
-    piece = w.shape[3:]
+    chips = w_own.shape[0]
+    sums = (2, cols) + w_own.shape
     DMA = pltpu.SemaphoreType.DMA
     return pl.pallas_call(
         functools.partial(finish_kernel, parts, cols),
         out_shape=(
             jax.ShapeDtypeStruct(shares.shape, BF16),
             jax.ShapeDtypeStruct(self_rows.shape, BF16),
-            jax.ShapeDtypeStruct(w.shape, BF16),
+            jax.ShapeDtypeStruct(sums, BF16),
         ),
-        in_specs=[ANY, ANY, VMEM],
+        in_specs=[ANY, ANY, VMEM, [VMEM] * len(w_in)],
         out_specs=(ANY, ANY, VMEM),
         scratch_shapes=[
-            pltpu.VMEM((cols, chips) + piece, F32),
-            pltpu.VMEM((cols, chips) + piece, BF16),
-            pltpu.VMEM((cols, chips) + piece, BF16),
-            pltpu.VMEM((chips,) + piece, BF16),
-            pltpu.VMEM((chips,) + piece, BF16),
-            pltpu.VMEM(w.shape, BF16),
+            pltpu.VMEM(w_own.shape, BF16),
+            pltpu.VMEM(w_own.shape, BF16),
+            pltpu.VMEM(sums, BF16),
             DMA((parts,)), DMA((parts,)), DMA((cols,)), DMA((cols,)), DMA,
-            DMA((2,)), DMA((2,)), DMA((2, cols)), DMA((2, cols)),
+            DMA, DMA, DMA((cols,)), DMA((cols,)),
             DMA((chips,)), DMA((chips,)), DMA((chips,)), DMA((chips,)),
         ],
         compiler_params=pltpu.CompilerParams(collective_id=1, has_side_effects=True, vmem_limit_bytes=40 << 20),
         name="finish",
-    )(shares, self_rows, w)
+    )(shares, self_rows, w_own, w_in)
 
 
 def combine_kernel(scale, wanted_ref, self_ref, own_ref, back_ref, sums_ref, out_ref, gs_ref, gn_ref):
@@ -506,16 +524,19 @@
     slots = parts * cap
     hid = width * cols
     scale = 1.0 / math.sqrt(node_rows * parts)
-    fetch = jnp.pad(fetch_ids.reshape(parts, 1, cap), ((0, 0), (0, 0), (0, 128 - cap)))
-    refs = colref.reshape(blocks * per_block)
+    fetch = jnp.pad(fetch_ids.reshape(parts, cap).T, ((0, 0), (0, 128 - parts)))
+    refs = colref.T
     gout = grad_out.reshape(blocks // cols, tile, hid)
-    act, self_rows, gagg, w, wanted = layer(
+    act, self_rows, gagg, w_own, w_send, wanted = layer(
         fetch, refs, feats.reshape(blocks, tile, width), adj_vals, w_self, w_neigh, gout, parts, cols, cap
     )
-    own, shares = spread(refs, adj_vals, gagg.reshape(blocks, tile, width), slots)
-    returned, self_part, sums = finish(shares.reshape(parts, cap, tile, width), self_rows, w)
+    w_in = [
+        lax.ppermute(w, "cols", [(c, (c + d) % cols) for c in range(cols)]) for d, w in enumerate(w_send, 1)
+    ]
+    own, shares, act = spread(refs, adj_vals, gagg.reshape(blocks, tile, width), act, slots)
+    returned, self_part, sums = finish(shares.reshape(parts, cap, tile, width), self_rows, w_own, w_in)
     grad_feats, grad_self, grad_neigh = combine(
-        wanted[:, 0, :cap].reshape(slots), self_part.reshape(blocks, tile, width), own,
+        wanted, self_part.reshape(blocks, tile, width), own,
         returned.reshape(slots, tile, width), sums, scale,
     )
     return act.reshape(grad_out.shape), grad_self, grad_neigh, grad_feats.reshape(node_rows, width)

time: 153 us -> 137 us (0.90)
  Pallas kernels: 146 us -> 128 us
  starting transfers between devices: 0 us -> 3.46 us
  local copies, waits for them, and re-layouts: 6.05 us -> 3.71 us
    pallas_call x1, Pallas kernels: 52.7 us -> 38.2 us  [finish(): pl.pallas_call(functools.partial(finish_kernel, parts, cols), out_shape=(...]
    pallas_call x1, Pallas kernels: 75.4 us -> 71.6 us  [layer(): pl.pallas_call(functools.partial(layer_kernel, parts, cols, cap, blocks,...]
    ppermute x0 -> x3, starting transfers between devices: none -> 3.46 us  [body(): lax.ppermute(w, 'cols', [(c, (c + d) % cols) for c in range(cols)])]
    unnamed x14 -> x12, local copies, waits for them, and re-layouts: 5.05 us -> 2.46 us
  transfers between devices with their start and end apart: 0 -> 3, of which waited for: 0 -> 0; matrix products, arithmetic and copies ran while one was open for 0% -> 0% of each run, Pallas kernels for 0% -> 11%
where the time goes in v3:
time: 137 us; the launch traced here: 136 us
  Pallas kernels  128 us (93%)
  local copies, waits for them, and re-layouts  3.71 us (3%)
  starting transfers between devices  3.46 us (3%)
    pallas_call x1, Pallas kernels, layer(): pl.pallas_call(functools.partial(layer_kernel, parts, cols, cap, blocks,...  71.6 us
    pallas_call x1, Pallas kernels, finish(): pl.pallas_call(functools.partial(finish_kernel, parts, cols), out_shape=(...  38.2 us
    pallas_call x1, Pallas kernels, spread(): pl.pallas_call(functools.partial(spread_kernel, per_step), grid=(blocks /...  14.5 us
    pallas_call x1, Pallas kernels, combine(): pl.pallas_call(functools.partial(combine_kernel, scale), out_shape=(jax.S...  4.03 us
    ppermute x3, starting transfers between devices, body(): lax.ppermute(w, 'cols', [(c, (c + d) % cols) for c in range(cols)])  3.46 us
  transfers between devices with their start and end apart: 3, of which 0 were waited for; matrix products, arithmetic and copies ran while one was open for 0% of the time, Pallas kernels for 11%

profile of v3, /device:TPU:1, one launch (start us, length us, event | category | flops | bytes accessed | tf_op | source)
XLA Modules:
  0.0 136.1 jit_solution(17167235724708116651)
XLA Ops:
  0.6 1.2 pad.4.fetch_ref
  1.9 0.0 copy-start.4
  1.9 71.6 %layer.1 = (bf16[8,128,512]{2,1,0:T(8,128)(2,1)}, bf16[4,8,128,128]{3,2,1,0:T(8,128)(2,1)}, bf16[4,8,128,128]{3,2,1,0:T(8,128)(2,1)}, f32[16,16,256]{2,1,0:T(8,1...) custom-call(s32[2,128]{1,0:T(2,128)} %pad.4.fetch_ref, ...), custom_call_target="tpu_custom_call" | custom-call | tf_op jit(solution)/shard_map/layer/pallas_call | solution.py:252
  73.4 0.1 collective-permute-start
  73.5 2.2 %collective-permute-start.1 = (bf16[16,16,256]{2,1,0:T(8,128)(2,1)}, bf16[16,16,256]{2,1,0:T(8,128)(2,1)S(1)}, u32[]{:S(2)}, u32[]{:S(2)}) collective-permute-start(bf16[16,16,256]{2,1,0:T(8,128)(2,1)} %get-tuple-element.29), channel_id=1, source_target_pairs={{0,2},{1,3},{2,0},{3,1},{4,6},{5,7},{6,4},{7,5},{8,10},{9,11},{10,... | collective-permute-start | bytes 393224 | tf_op jit(solution)/shard_map/ppermute | solution.py:534
  75.7 1.2 collective-permute-start.2
  76.9 0.0 copy-done.4
  76.9 0.0 copy-start
  76.9 1.2 copy-done
  78.1 0.0 copy-start.1
  78.1 1.2 copy-done.1
  79.4 0.0 copy-start.2
  79.4 0.0 copy-start.3
  79.4 14.5 %spread.1 = (bf16[32,128,128]{2,1,0:T(8,128)(2,1)S(1)}, bf16[64,128,128]{2,1,0:T(8,128)(2,1)S(1)}, bf16[8,128,512]{2,1,0:T(8,128)(2,1)}) custom-call(s32[16,32]{1,0:T(8,128)S(1)} %bitcast.17, bf16[32,16,128,128]{3,2,1,0:T(8,128)(2,1)} %adj_ref.1, bf16[32,128,128]{2,1,0:T(8,128)(2,1)S(1)} %bitcast.14, bf16[8,128,512]{2,1,0:T(8,128)(2,1)S(1)} %copy-done), custom_call_target="tpu_custom_call" | custom-call | flops 2147483648 | bytes 16777216 | tf_op jit(solution)/shard_map/spread/pallas_call | solution.py:330
  93.9 0.0 copy-start.5
  93.9 0.0 collective-permute-done.w_refs_0_
  93.9 0.0 collective-permute-done.1.w_refs_1_
  93.9 0.0 collective-permute-done.2.w_refs_2_
  93.9 0.0 copy-done.2
  93.9 0.0 copy-done.3
  93.9 38.2 %finish.1 = (bf16[32,2,128,128]{3,2,1,0:T(8,128)(2,1)S(1)}, bf16[4,8,128,128]{3,2,1,0:T(8,128)(2,1)S(1)}, bf16[2,4,16,16,256]{4,3,2,1,0:T(8,128)(2,1)S(1)}) custom-call(bf16[32,2,128,128]{3,2,1,0:T(8,128)(2,1)S(1)} %bitcast.12, bf16[4,8,128,128]{3,2,1,0:T(8,128)(2,1)S(1)} %copy-done.2, f32[16,16,256]{2,1,0:T(8,128)S(1)} %copy-done.3, ...), custom_call_target="tpu_custom_call" | custom-call | tf_op jit(solution)/shard_map/finish/pallas_call | solution.py:459
  132.1 0.0 copy-done.5
  132.1 4.0 %combine.1 = (f32[32,128,128]{2,1,0:T(8,128)}, f32[512,512]{1,0:T(8,128)}, f32[512,512]{1,0:T(8,128)}) custom-call(s32[64]{0:T(128)S(1)} %copy-done.5, bf16[32,128,128]{2,1,0:T(8,128)(2,1)S(1)} %bitcast.15, bf16[32,128,128]{2,1,0:T(8,128)(2,1)S(1)} %get-tuple-element.32.own_ref, bf16[64,128,128]{2,1,0:T(8,128)(2,1)S(1)} %bitcast.13, ...), custom_call_target="tpu_custom_call" | custom-call | tf_op jit(solution)/shard_map/combine/pallas_call | solution.py:508
Async XLA Ops:
  1.9 75.0 %copy-start.4 = (s32[32,16]{0,1:T(8,128)S(1)}, s32[32,16]{0,1:T(8,128)}, u32[]{:S(2)}) copy-start(s32[32,16]{0,1:T(8,128)} %param.9) | copy-start | bytes 6148
  73.4 20.4 %collective-permute-start = (bf16[16,16,256]{2,1,0:T(8,128)(2,1)}, bf16[16,16,256]{2,1,0:T(8,128)(2,1)S(1)}, u32[]{:S(2)}, u32[]{:S(2)}) collective-permute-start(bf16[16,16,256]{2,1,0:T(8,128)(2,1)} %get-tuple-element.28), channel_id=1, source_target_pairs={{0,1},{1,2},{2,3},{3,0},{4,5},{5,6},{6,7},{7,4},{8,9},{9,10},{10,1... | collective-permute-start | bytes 393224 | tf_op jit(solution)/shard_map/ppermute | solution.py:534
  73.5 20.4 %collective-permute-start.1 = (bf16[16,16,256]{2,1,0:T(8,128)(2,1)}, bf16[16,16,256]{2,1,0:T(8,128)(2,1)S(1)}, u32[]{:S(2)}, u32[]{:S(2)}) collective-permute-start(bf16[16,16,256]{2,1,0:T(8,128)(2,1)} %get-tuple-element.29), channel_id=1, source_target_pairs={{0,2},{1,3},{2,0},{3,1},{4,6},{5,7},{6,4},{7,5},{8,10},{9,11},{10,... | collective-permute-start | bytes 393224 | tf_op jit(solution)/shard_map/ppermute | solution.py:534
  75.7 18.2 %collective-permute-start.2 = (bf16[16,16,256]{2,1,0:T(8,128)(2,1)}, bf16[16,16,256]{2,1,0:T(8,128)(2,1)S(1)}, u32[]{:S(2)}, u32[]{:S(2)}) collective-permute-start(bf16[16,16,256]{2,1,0:T(8,128)(2,1)} %get-tuple-element.30), channel_id=1, source_target_pairs={{0,3},{1,0},{2,1},{3,2},{4,7},{5,4},{6,5},{7,6},{8,11},{9,8},{10,9... | collective-permute-start | bytes 393224 | tf_op jit(solution)/shard_map/ppermute | solution.py:534
  76.9 1.2 copy-start
  78.1 1.2 copy-start.1
  79.4 14.5 %copy-start.2 = (bf16[4,8,128,128]{3,2,1,0:T(8,128)(2,1)S(1)}, bf16[4,8,128,128]{3,2,1,0:T(8,128)(2,1)}, u32[]{:S(2)}) copy-start(bf16[4,8,128,128]{3,2,1,0:T(8,128)(2,1)} %get-tuple-element.26.self_hbm) | copy-start | bytes 3145732
  79.4 14.5 %copy-start.3 = (f32[16,16,256]{2,1,0:T(8,128)S(1)}, f32[16,16,256]{2,1,0:T(8,128)}, u32[]{:S(2)}) copy-start(f32[16,16,256]{2,1,0:T(8,128)} %get-tuple-element.27.w_own_ref) | copy-start | bytes 786436
  93.9 38.2 %copy-start.5 = (s32[64]{0:T(128)S(1)}, s32[64]{0:T(128)}, u32[]{:S(2)}) copy-start(s32[64]{0:T(128)} %get-tuple-element.24.wanted_ref) | copy-start | bytes 772

commit v4 on v3

v4 whole, which is shorter than its diff:
```python
import functools
import math

import jax
import jax.numpy as jnp
from jax import lax
from jax.experimental import pallas as pl
from jax.experimental.pallas import tpu as pltpu
from jax.sharding import PartitionSpec as P

MESH = pl.DeviceIdType.MESH
ANY = pl.BlockSpec(memory_space=pl.ANY)
VMEM = pl.BlockSpec(memory_space=pltpu.VMEM)
SMEM = pl.BlockSpec(memory_space=pltpu.SMEM)
BF16 = jnp.bfloat16
F32 = jnp.float32


def remote(src, dst, send, recv, axis, peer):
    return pltpu.make_async_remote_copy(
        src_ref=src, dst_ref=dst, send_sem=send, recv_sem=recv,
        device_id={axis: peer}, device_id_type=MESH,
    )


def send_order(parts):
    side = math.isqrt(parts // 2)
    hops = lambda n: min(n, side - n)
    offsets = [(y, x, c) for y in range(side) for x in range(side) for c in range(2)][1:]
    return sorted(offsets, key=lambda o: (-hops(o[0]) - hops(o[1]), o[2]))


def at_offset(me, parts, offset):
    side = math.isqrt(parts // 2)
    dy, dx, dc = offset
    core, chip = lax.rem(me, 2), me // 2
    y, x = lax.rem(chip // side + dy, side), lax.rem(lax.rem(chip, side) + dx, side)
    return (y * side + x) * 2 + (1 - core if dc else core)


def layer_kernel(parts, cols, cap, blocks, per_block, step, fetch_ref, colref_ref, slots_ref, feats_hbm, adj_hbm,
                 w_self_hbm, w_neigh_hbm, gout_hbm, act_ref, selfp_hbm, ret_hbm, own_ref, sums_ref, wanted_ref,
                 pool, own_v, adj_v, stage, agg_v, frows, arows, w_v, gout_v, gagg_v, gagg_in, self_v, gw, from_core, w_half,
                 w_out, w_in, to_chip, from_chip, sums, run_v, sort_v, sort_s, idx_v, idx_s,
                 pool_sem, adj_sem, own_sem, ownv_sem, w_sem, gout_sem, smem_sem, sort_sem,
                 idx_send, idx_recv, tile_send, tile_recv, f_send, f_recv, a_send, a_recv, g_send, g_recv,
                 core_send, core_recv, wz_send, wz_recv, s_send, s_recv, p_send, p_recv,
                 z_send, z_recv, chip_send, chip_recv, up_send, up_recv, pair_send, pair_recv):
    me = lax.axis_index("rows")
    mc = lax.axis_index("cols")
    share = blocks // cols
    groups = share // step
    tile, width = own_v.shape[1:]
    hid = cols * width

    local = [
        pltpu.make_async_copy(feats_hbm, own_v, ownv_sem),
        pltpu.make_async_copy(feats_hbm, pool.at[pl.ds(0, blocks)], pool_sem),
        pltpu.make_async_copy(feats_hbm.at[pl.ds(mc * share, share)], frows.at[mc], own_sem),
        pltpu.make_async_copy(w_self_hbm, w_v.at[pl.ds(0, hid)], w_sem.at[0]),
        pltpu.make_async_copy(w_neigh_hbm, w_v.at[pl.ds(hid, hid)], w_sem.at[1]),
        pltpu.make_async_copy(gout_hbm, gout_v, gout_sem),
    ]
    for q in range(cols):
        part = pl.ds(q * share * per_block, share * per_block)
        local.append(pltpu.make_async_copy(adj_hbm.at[part], adj_v.at[part], adj_sem.at[q]))
    local[0].start()

    barrier = pltpu.get_barrier_semaphore()

    def hello(d, _):
        pl.semaphore_signal(barrier, inc=1, device_id={"rows": lax.rem(me + d, parts)}, device_id_type=MESH)
        return 0

    lax.fori_loop(1, parts, hello, 0)
    for d in range(1, cols):
        pl.semaphore_signal(barrier, inc=1, device_id={"cols": lax.rem(mc + d, cols)}, device_id_type=MESH)
    pl.semaphore_wait(barrier, parts - 1 + cols - 1)

    def ask(d, _):
        p = lax.rem(me + d, parts)
        remote(fetch_ref, idx_v.at[me], idx_send.at[p], idx_recv.at[me], "rows", p).start()
        return 0

    lax.fori_loop(1, parts, ask, 0)
    idx_v[me] = jnp.full(idx_v.shape[1:], -1, jnp.int32)
    local[0].wait()

    def asked(d, _):
        p = lax.rem(me + parts - d, parts)
        remote(fetch_ref, idx_v.at[p], idx_send.at[p], idx_recv.at[p], "rows", p).wait_recv()
        return 0

    lax.fori_loop(1, parts, asked, 0)
    to_smem = pltpu.make_async_copy(idx_v, idx_s, smem_sem)
    to_smem.start()
    to_smem.wait()
    for offset in send_order(parts):
        p = at_offset(me, parts, offset)
        for s in range(cap):
            stage[p, s] = own_v[jnp.maximum(idx_s[p, s, me], 0)]
        remote(stage.at[p], pool.at[pl.ds(blocks + me * cap, cap)], tile_send.at[p], tile_recv.at[me], "rows", p).start()

    for d in range(1, cols):
        p = lax.rem(mc + d, cols)
        remote(own_v.at[pl.ds(p * share, share)], frows.at[mc], f_send.at[p], f_recv.at[mc], "cols", p).start()
    for copy in local[1:]:
        copy.start()

    def want(p, _):
        for s in range(cap):
            wanted_ref[p * cap + s] = idx_s[p, s, me]
        return 0

    lax.fori_loop(0, parts, want, 0)

    refs = blocks * per_block
    key_row = slots_ref[...] * refs + lax.broadcasted_iota(jnp.int32, (1, refs), 1)
    down = lax.broadcasted_iota(jnp.int32, (refs, refs), 0)
    across = lax.broadcasted_iota(jnp.int32, (refs, refs), 1)
    key_col = jnp.sum(jnp.where(down == across, key_row, 0), axis=1, keepdims=True)
    rank_col = jnp.sum(jnp.where(key_row < key_col, 1, 0), axis=1, keepdims=True)
    sort_v[0:1, :] = jnp.sum(jnp.where(rank_col == across, down, 0), axis=0, keepdims=True)
    before = jnp.where(key_col < (across + 1) * refs, 1, 0)
    sort_v[1:2, :] = jnp.sum(before, axis=0, keepdims=True) - 1
    sort_v[2:3, :] = jnp.sum(jnp.where(key_col < across * refs, 0, before), axis=0, keepdims=True)
    to_sort = pltpu.make_async_copy(sort_v, sort_s, sort_sem)
    to_sort.start()
    to_sort.wait()

    pool[pl.ds(blocks + me * cap, cap)] = jnp.zeros((cap,) + pool.shape[1:], BF16)
    for copy in local[1:]:
        copy.wait()
    for d in range(1, cols):
        p = lax.rem(mc + d, cols)
        remote(own_v.at[pl.ds(p * share, share)], frows.at[p], f_send.at[p], f_recv.at[p], "cols", p).wait()

    def given(d, _):
        p = lax.rem(me + parts - d, parts)
        remote(stage.at[p], pool.at[pl.ds(blocks + p * cap, cap)], tile_send.at[p], tile_recv.at[p], "rows", p).wait_recv()
        return 0

    lax.fori_loop(1, parts, given, 0)

    def aggregate(b):
        left = jnp.concatenate([adj_v[b * per_block + k] for k in range(per_block)], axis=1)
        right = jnp.concatenate([pool[colref_ref[k, b]] for k in range(per_block)], axis=0)
        return jnp.dot(left, right, preferred_element_type=F32).astype(BF16)

    def agg_copy(p, slot, i):
        return remote(agg_v.at[p, i], arows.at[slot, i], a_send.at[p, i], a_recv.at[slot, i], "cols", p)

    def back_copy(p, slot, g):
        part = pl.ds(g * step, step)
        return remote(gagg_v.at[p, part], gagg_in.at[slot, part], g_send.at[p, g], g_recv.at[slot, g], "cols", p)

    def tile_round(i):
        def one(d, _):
            p = lax.rem(mc + d, cols)
            agg_v[p, i] = aggregate(p * share + i)
            agg_copy(p, mc, i).start()
            return 0

        lax.fori_loop(1, cols, one, 0)
        arows[mc, i] = aggregate(mc * share + i)

    def dense(g):
        part = pl.ds(g * step, step)
        for j in range(step):
            for d in range(1, cols):
                p = lax.rem(mc + d, cols)
                agg_copy(p, p, g * step + j).wait_recv()

        def rows_of(ref):
            return jnp.concatenate([ref[c, part].reshape(step * tile, width) for c in range(cols)], axis=1)

        both = jnp.concatenate([rows_of(frows), rows_of(arows)], axis=1)
        v = jnp.dot(both, w_v[...], preferred_element_type=F32)
        c0 = math.sqrt(2.0 / math.pi)
        v2 = v * v
        t = jnp.tanh(c0 * v * (1.0 + 0.044715 * v2))
        half = 0.5 * (1.0 + t)
        act_ref[part] = (v * half).astype(BF16).reshape(step, tile, hid)
        slope = half + (0.5 * v) * (1.0 - t * t) * (c0 * (1.0 + 3.0 * 0.044715 * v2))
        grad_pre = (gout_v[part].reshape(step * tile, hid).astype(F32) * slope).astype(BF16)
        nt = (((1,), (1,)), ((), ()))
        out = lax.dot_general(grad_pre, w_v[pl.ds(hid, hid)], nt, preferred_element_type=F32).astype(BF16)
        for c in range(cols):
            gagg_v[c, part] = out[:, c * width:(c + 1) * width].reshape(step, tile, width)
        for d in range(1, cols):
            back_copy(lax.rem(mc + d, cols), mc, g).start()
        gagg_in[mc, part] = gagg_v[mc, part]
        out = lax.dot_general(grad_pre, w_v[pl.ds(0, hid)], nt, preferred_element_type=F32).astype(BF16)
        for c in range(cols):
            self_v[c, part] = out[:, c * width:(c + 1) * width].reshape(step, tile, width)
        sums = lax.dot_general(both, grad_pre, (((0,), (0,)), ((), ())), preferred_element_type=F32)
        gw[...] += sums.reshape(gw.shape)

    def spread(g):
        for d in range(1, cols):
            p = lax.rem(mc + d, cols)
            back_copy(p, p, g).wait_recv()

        def one(n, _):
            c, i = n // step, g * step + lax.rem(n, step)
            at = (c * share + i) * per_block
            grad_t = gagg_in[c, i].T
            for k in range(0, per_block, 2):
                pair = jnp.concatenate([adj_v[at + k], adj_v[at + k + 1]], axis=1)
                out = jnp.dot(grad_t, pair, preferred_element_type=F32).astype(BF16)
                adj_v[at + k] = out[:, :tile]
                adj_v[at + k + 1] = out[:, tile:]
            return 0

        lax.fori_loop(0, cols * step, one, 0)

    gw[...] = jnp.zeros_like(gw)

    def work(g, _):
        @pl.when(g < groups)
        def _():
            for j in range(step):
                tile_round(g * step + j)

        @pl.when((g > 0) & (g <= groups))
        def _():
            dense(g - 1)

        @pl.when(g > 1)
        def _():
            spread(g - 2)

        return 0

    lax.fori_loop(0, groups + 1, work, 0)

    core = lax.rem(me, 2)
    mate = me + 1 - 2 * core
    pair = remote(gw.at[1 - core], from_core, core_send, core_recv, "rows", mate)
    pair.start()
    work(groups + 1, 0)

    def share_copy(p, slot):
        return remote(stage.at[p], ret_hbm.at[slot], s_send.at[p], s_recv.at[slot], "rows", p)

    def self_copy(p, slot):
        return remote(self_v.at[p], selfp_hbm.at[slot], p_send.at[p], p_recv.at[slot], "cols", p)

    def others():
        return [lax.rem(mc + d, cols) for d in range(1, cols)]

    chips = parts // 2
    chip = me // 2

    def over_chips(f):
        def one(d, _):
            f(lax.rem(chip + d, chips))
            return 0

        lax.fori_loop(1, chips, one, 0)

    pair.wait()
    _, _, rows_p, cols_p = w_half.shape
    wide = hid // cols_p
    for c in range(cols):
        for q in range(chips):
            rows = pl.ds(c * (hid // cols) + (q // wide) * rows_p, rows_p)
            lanes = pl.ds((q % wide) * cols_p, cols_p)
            w_half[c, q] = gw[core, rows, lanes] + from_core[rows, lanes]
        w_out[c] = w_half[c].astype(BF16)

    def wz_copy(p, slot):
        return remote(w_out.at[p], w_in.at[slot], wz_send.at[p], wz_recv.at[slot], "cols", p)

    for p in others():
        wz_copy(p, mc).start()
    for p in others():
        self_copy(p, mc).start()
    own_self = pltpu.make_async_copy(self_v.at[mc], selfp_hbm.at[mc], own_sem)
    own_self.start()

    def run(n, carry):
        last_slot, total = carry
        ref = sort_s[0, n]
        slot = colref_ref[lax.rem(ref, per_block), ref // per_block]
        total = jnp.where(slot == last_slot, total, 0.0) + adj_v[ref].astype(F32)
        run_v[n] = total.astype(BF16)
        return slot, total

    lax.fori_loop(0, refs, run, (jnp.int32(-1), jnp.zeros((width, tile), F32)), unroll=4)

    def drain_tiles(d, _):
        p = lax.rem(me + d, parts)
        remote(stage.at[p], pool.at[pl.ds(blocks + p * cap, cap)], tile_send.at[p], tile_recv.at[p], "rows", p).wait_send()
        return 0

    lax.fori_loop(1, parts, drain_tiles, 0)

    def share_of(slot):
        tile_sum = run_v[jnp.maximum(sort_s[1, slot], 0)]
        return jnp.where(sort_s[2, slot] > 0, tile_sum, jnp.zeros_like(tile_sum))

    order = send_order(parts)

    def shares(lo, hi):
        for offset in order[lo:hi]:
            p = at_offset(me, parts, offset)
            for n in range(cap):
                stage[p, n] = share_of(blocks + p * cap + n)
            share_copy(p, me).start()

    for p in others():
        wz_copy(p, p).wait()
    total = w_half[mc]
    for p in others():
        total = total + w_in[p].astype(F32)
    to_chip[...] = total.astype(BF16)

    def chip_copy(q, slot):
        return remote(to_chip.at[q], from_chip.at[slot], chip_send.at[q], chip_recv.at[slot], "rows", 2 * q + core)

    over_chips(lambda q: chip_copy(q, chip).start())
    shares(0, 8)
    from_chip[chip] = to_chip[chip]
    over_chips(lambda q: chip_copy(q, q).wait())
    total = from_chip[0].astype(F32)
    for q in range(1, chips):
        total = total + from_chip[q].astype(F32)
    sums[core, mc, chip] = total.astype(BF16)

    def up_copy(q, slot):
        return remote(sums.at[core, mc, chip], sums.at[core, mc, slot], up_send.at[q], up_recv.at[slot], "rows", 2 * q + core)

    over_chips(lambda q: up_copy(q, chip).start())
    shares(8, 18)
    over_chips(lambda q: up_copy(q, q).wait())

    def z_up(p, slot):
        return remote(sums.at[core, mc], sums.at[core, slot], z_send.at[p], z_recv.at[slot], "cols", p)

    for p in others():
        z_up(p, mc).start()
    shares(18, parts - 1)

    def own_share(t, _):
        own_ref[t] = share_of(t)
        return 0

    lax.fori_loop(0, blocks, own_share, 0)
    for p in others():
        z_up(p, p).wait()
    pair_up = remote(sums.at[core], sums.at[core], pair_send, pair_recv, "rows", mate)
    pair_up.start()
    pair_up.wait()
    sums_ref[...] = sums[...]

    for p in others():
        self_copy(p, p).wait()
    own_self.wait()

    def drain(d, _):
        p = lax.rem(me + d, parts)
        remote(fetch_ref, idx_v.at[p], idx_send.at[p], idx_recv.at[p], "rows", p).wait_send()
        share_copy(p, p).wait()
        return 0

    lax.fori_loop(1, parts, drain, 0)

    def drain_agg(i, _):
        for d in range(1, cols):
            p = lax.rem(mc + d, cols)
            agg_copy(p, p, i).wait_send()
        return 0

    lax.fori_loop(0, share, drain_agg, 0)

    def drain_back(g, _):
        for d in range(1, cols):
            p = lax.rem(mc + d, cols)
            back_copy(p, p, g).wait_send()
        return 0

    lax.fori_loop(0, groups, drain_back, 0)


def layer(fetch, colref, slots, feats, adj, w_self, w_neigh, gout, parts, cols, cap):
    refs, tile, _ = adj.shape
    blocks = feats.shape[0]
    per_block = refs // blocks
    width = feats.shape[-1]
    share = blocks // cols
    hid = cols * width
    step = 2
    groups = share // step
    chips = parts // 2
    piece = (16, 2 * hid * hid // (2 * cols * chips * 16))
    DMA = pltpu.SemaphoreType.DMA
    rows_shape = (cols, share, tile, width)
    return pl.pallas_call(
        functools.partial(layer_kernel, parts, cols, cap, blocks, per_block, step),
        out_shape=(
            jax.ShapeDtypeStruct(gout.shape, BF16),
            jax.ShapeDtypeStruct(rows_shape, BF16),
            jax.ShapeDtypeStruct((parts, cap, width, tile), BF16),
            jax.ShapeDtypeStruct((blocks, width, tile), BF16),
            jax.ShapeDtypeStruct((2, cols, chips) + piece, BF16),
            jax.ShapeDtypeStruct((parts * cap,), jnp.int32),
        ),
        in_specs=[VMEM, SMEM, VMEM, ANY, ANY, ANY, ANY, ANY],
        out_specs=(VMEM, ANY, ANY, VMEM, VMEM, SMEM),
        scratch_shapes=[
            pltpu.VMEM((blocks + parts * cap, tile, width), BF16),
            pltpu.VMEM(feats.shape, BF16),
            pltpu.VMEM(adj.shape, BF16),
            pltpu.VMEM((parts, cap, tile, width), BF16),
            pltpu.VMEM(rows_shape, BF16),
            pltpu.VMEM(rows_shape, BF16),
            pltpu.VMEM(rows_shape, BF16),
            pltpu.VMEM((2 * hid, hid), BF16),
            pltpu.VMEM(gout.shape, BF16),
            pltpu.VMEM(rows_shape, BF16),
            pltpu.VMEM(rows_shape, BF16),
            pltpu.VMEM(rows_shape, BF16),
            pltpu.VMEM((2, hid, hid), F32),
            pltpu.VMEM((hid, hid), F32),
            pltpu.VMEM((cols, chips) + piece, F32),
            pltpu.VMEM((cols, chips) + piece, BF16),
            pltpu.VMEM((cols, chips) + piece, BF16),
            pltpu.VMEM((chips,) + piece, BF16),
            pltpu.VMEM((chips,) + piece, BF16),
            pltpu.VMEM((2, cols, chips) + piece, BF16),
            pltpu.VMEM((refs, width, tile), BF16),
            pltpu.VMEM((8, refs), jnp.int32),
            pltpu.SMEM((8, refs), jnp.int32),
            pltpu.VMEM((parts,) + fetch.shape, jnp.int32),
            pltpu.SMEM((parts,) + fetch.shape, jnp.int32),
            DMA, DMA((cols,)), DMA, DMA, DMA((2,)), DMA, DMA, DMA,
            DMA((parts,)), DMA((parts,)), DMA((parts,)), DMA((parts,)),
            DMA((cols,)), DMA((cols,)), DMA((cols, share)), DMA((cols, share)),
            DMA((cols, groups)), DMA((cols, groups)), DMA, DMA,
            DMA((cols,)), DMA((cols,)), DMA((parts,)), DMA((parts,)), DMA((cols,)), DMA((cols,)),
            DMA((cols,)), DMA((cols,)), DMA((chips,)), DMA((chips,)), DMA((chips,)), DMA((chips,)), DMA, DMA,
        ],
        compiler_params=pltpu.CompilerParams(collective_id=0, has_side_effects=True, vmem_limit_bytes=63 << 20),
        name="layer",
    )(fetch, colref, slots, feats, adj, w_self, w_neigh, gout)


def combine_kernel(scale, wanted_ref, self_ref, own_ref, back_ref, sums_ref, act_ref,
                   out_ref, gs_ref, gn_ref, act_out_ref, total):
    slots = back_ref.shape[0]
    act_out_ref[...] = act_ref[...]
    total[...] = own_ref[...].astype(F32)

    def add(s, _):
        t = wanted_ref[s]

        @pl.when(t >= 0)
        def _():
            total[t] += back_ref[s].astype(F32)

        return 0

    lax.fori_loop(0, slots, add, 0)

    def put(t, _):
        out_ref[t] = self_ref[t].astype(F32) + total[t].T
        return 0

    lax.fori_loop(0, total.shape[0], put, 0, unroll=4)
    halves, cols, chips, rows_p, cols_p = sums_ref.shape
    hid = gs_ref.shape[0]
    wide = hid // cols_p
    for half, ref in enumerate((gs_ref, gn_ref)):
        for c in range(cols):
            for q in range(chips):
                at = c * (hid // cols) + (q // wide) * rows_p
                ref[at:at + rows_p, (q % wide) * cols_p:(q % wide + 1) * cols_p] = sums_ref[half, c, q].astype(F32) * scale


def combine(wanted, self_part, own, back, sums, act, scale):
    hid = self_part.shape[-1] * sums.shape[1]
    weights = jax.ShapeDtypeStruct((hid, hid), F32)
    return pl.pallas_call(
        functools.partial(combine_kernel, scale),
        out_shape=(jax.ShapeDtypeStruct(self_part.shape, F32), weights, weights, jax.ShapeDtypeStruct(act.shape, BF16)),
        in_specs=[SMEM, VMEM, VMEM, VMEM, VMEM, VMEM],
        out_specs=(VMEM, VMEM, VMEM, VMEM),
        scratch_shapes=[pltpu.VMEM(own.shape, F32)],
        compiler_params=pltpu.CompilerParams(vmem_limit_bytes=40 << 20),
        name="combine",
    )(wanted, self_part, own, back, sums, act)


def body(feats, adj_vals, colref, fetch_ids, w_self, w_neigh, grad_out):
    node_rows, width = feats.shape
    blocks, per_block, tile, _ = adj_vals.shape
    parts = lax.axis_size("rows")
    cols = lax.axis_size("cols")
    cap = fetch_ids.shape[2]
    refs = blocks * per_block
    hid = width * cols
    scale = 1.0 / math.sqrt(node_rows * parts)
    fetch = jnp.pad(fetch_ids.reshape(parts, cap).T, ((0, 0), (0, 128 - parts)))
    gout = grad_out.reshape(blocks // cols, tile, hid)
    act, self_part, returned, own, sums, wanted = layer(
        fetch, colref.T, colref.reshape(1, refs), feats.reshape(blocks, tile, width),
        adj_vals.reshape(refs, tile, tile), w_self, w_neigh, gout, parts, cols, cap,
    )
    grad_feats, grad_self, grad_neigh, act = combine(
        wanted, self_part.reshape(blocks, tile, width), own, returned.reshape(parts * cap, width, tile), sums, act, scale
    )
    return act.reshape(grad_out.shape), grad_self, grad_neigh, grad_feats.reshape(node_rows, width)


def solution(mesh):
    in_specs = (
        P("rows", "cols"),
        P("rows", None, None, None),
        P("rows", None),
        P("rows", None, None),
        P(),
        P(),
        P(("rows", "cols"), None),
    )
    out_specs = (P(("rows", "cols"), None), P(), P(), P("rows", "cols"))
    return jax.shard_map(body, mesh=mesh, in_specs=in_specs, out_specs=out_specs, check_vma=False)
```

time: 137 us -> 133 us (0.971)
  local copies, waits for them, and re-layouts: 3.71 us -> 9.74 us
  Pallas kernels: 128 us -> 122 us
  starting transfers between devices: 3.46 us -> 0 us
    pallas_call x2 -> x0, Pallas kernels: 52.7 us -> none  [the longest x1 38.2 us: finish(): pl.pallas_call(functools.partial(finish_kernel, parts, cols), out_shape=(...]
    pallas_call x1, Pallas kernels: 71.6 us -> 117 us  [layer(): pl.pallas_call(functools.partial(layer_kernel, parts, cols, cap, blocks,...]
    unnamed x12 -> x13, local copies, waits for them, and re-layouts: 2.46 us -> 7.83 us
    ppermute x3 -> x0, starting transfers between devices: 3.46 us -> none  [body(): lax.ppermute(w, 'cols', [(c, (c + d) % cols) for c in range(cols)])]
  transfers between devices with their start and end apart: 3 -> 0, of which waited for: 0 -> 0; matrix products, arithmetic and copies ran while one was open for 0% -> 0% of each run, Pallas kernels for 11% -> 0%
where the time goes in v4:
time: 133 us; the launch traced here: 132 us
  Pallas kernels  122 us (92%)
  local copies, waits for them, and re-layouts  9.74 us (7%)
    pallas_call x1, Pallas kernels, layer(): pl.pallas_call(functools.partial(layer_kernel, parts, cols, cap, blocks,...  117 us
    unnamed x13, local copies, waits for them, and re-layouts  7.83 us
    pallas_call x1, Pallas kernels, combine(): pl.pallas_call(functools.partial(combine_kernel, scale), out_shape=(jax.S...  5.18 us

profile of v4, /device:TPU:1, one launch (start us, length us, event | category | flops | bytes accessed | tf_op | source)
XLA Modules:
  0.0 132.2 jit_solution(2211890700700825696)
XLA Ops:
  0.6 1.2 pad.4.fetch_ref
  1.9 0.8 copy.12
  2.6 0.7 reshape.36.slots_ref
  3.3 116.7 %layer.1 = (bf16[8,128,512]{2,1,0:T(8,128)(2,1)}, bf16[4,8,128,128]{3,2,1,0:T(8,128)(2,1)}, bf16[32,2,128,128]{3,2,1,0:T(8,128)(2,1)}, bf16[32,128,128]{2,1,0:T(...) custom-call(s32[2,128]{1,0:T(2,128)} %pad.4.fetch_ref, s32[16,32]{1,0:T(8,128)} %bitcast.16, ...), custom_call_target="tpu_custom_call" | custom-call | tf_op jit(solution)/shard_map/layer/pallas_call | solution.py:399
  120.0 0.0 copy-start
  120.0 1.6 %copy-done = bf16[32,2,128,128]{3,2,1,0:T(8,128)(2,1)S(1)} copy-done((bf16[32,2,128,128]{3,2,1,0:T(8,128)(2,1)S(1)}, bf16[32,2,128,128]{3,2,1,0:T(8,128)(2,1)}, u32[]{:S(2)}) %copy-start) | copy-done | bytes 2097176
  121.6 0.0 copy-start.1
  121.6 1.2 copy-done.1
  122.8 0.0 copy-start.2
  122.8 1.2 copy-done.2
  124.0 0.0 copy-start.3
  124.0 1.2 copy-done.3
  125.3 0.0 copy-start.4
  125.3 1.2 copy-done.4
  126.5 0.0 copy-start.5
  126.5 0.6 copy-done.5
  127.1 5.2 %combine.1 = (f32[32,128,128]{2,1,0:T(8,128)}, f32[512,512]{1,0:T(8,128)}, f32[512,512]{1,0:T(8,128)}, bf16[8,128,512]{2,1,0:T(8,128)(2,1)}) custom-call(s32[64]{0:T(128)S(1)} %copy-done.5, bf16[32,128,128]{2,1,0:T(8,128)(2,1)S(1)} %bitcast.12, bf16[32,128,128]{2,1,0:T(8,128)(2,1)S(1)} %copy-done.3, bf16[64,128,128]{2,1,0:T(8,128)(2,1)S(1)} %bitcast.11, ...), custom_call_target="tpu_custom_call" | custom-call | tf_op jit(solution)/shard_map/combine/pallas_call | solution.py:484
Async XLA Ops:
  120.0 1.6 %copy-start = (bf16[32,2,128,128]{3,2,1,0:T(8,128)(2,1)S(1)}, bf16[32,2,128,128]{3,2,1,0:T(8,128)(2,1)}, u32[]{:S(2)}) copy-start(bf16[32,2,128,128]{3,2,1,0:T(8,128)(2,1)} %get-tuple-element.17) | copy-start | bytes 6291460
  121.6 1.2 copy-start.1
  122.8 1.2 copy-start.2
  124.0 1.2 copy-start.3
  125.3 1.2 copy-start.4
  126.5 0.6 copy-start.5

commit v5 on v4

--- a/solution.py
+++ b/solution.py
@@ -39,8 +39,8 @@
 
 
 def layer_kernel(parts, cols, cap, blocks, per_block, step, fetch_ref, colref_ref, slots_ref, feats_hbm, adj_hbm,
-                 w_self_hbm, w_neigh_hbm, gout_hbm, act_ref, selfp_hbm, ret_hbm, own_ref, sums_ref, wanted_ref,
-                 pool, own_v, adj_v, stage, agg_v, frows, arows, w_v, gout_v, gagg_v, gagg_in, self_v, gw, from_core, w_half,
+                 w_self_hbm, w_neigh_hbm, gout_hbm, act_hbm, selfp_hbm, ret_hbm, own_hbm, sums_ref, wanted_ref,
+                 act_v, pool, own_v, adj_v, stage, agg_v, frows, arows, w_v, gout_v, gagg_v, gagg_in, self_v, gw, from_core, w_half,
                  w_out, w_in, to_chip, from_chip, sums, run_v, sort_v, sort_s, idx_v, idx_s,
                  pool_sem, adj_sem, own_sem, ownv_sem, w_sem, gout_sem, smem_sem, sort_sem,
                  idx_send, idx_recv, tile_send, tile_recv, f_send, f_recv, a_send, a_recv, g_send, g_recv,
@@ -115,7 +115,14 @@
     lax.fori_loop(0, parts, want, 0)
 
     refs = blocks * per_block
-    key_row = slots_ref[...] * refs + lax.broadcasted_iota(jnp.int32, (1, refs), 1)
+    grid = (per_block, refs)
+    place = lax.broadcasted_iota(jnp.int32, grid, 1)
+    slots = jnp.zeros(grid, jnp.int32)
+    table = slots_ref[...]
+    for b in range(blocks):
+        slots = jnp.where(place // per_block == b, table[:, b:b + 1], slots)
+    slots = jnp.where(lax.rem(place, per_block) == lax.broadcasted_iota(jnp.int32, grid, 0), slots, 0)
+    key_row = jnp.sum(slots, axis=0, keepdims=True) * refs + lax.broadcasted_iota(jnp.int32, (1, refs), 1)
     down = lax.broadcasted_iota(jnp.int32, (refs, refs), 0)
     across = lax.broadcasted_iota(jnp.int32, (refs, refs), 1)
     key_col = jnp.sum(jnp.where(down == across, key_row, 0), axis=1, keepdims=True)
@@ -180,7 +187,7 @@
         v2 = v * v
         t = jnp.tanh(c0 * v * (1.0 + 0.044715 * v2))
         half = 0.5 * (1.0 + t)
-        act_ref[part] = (v * half).astype(BF16).reshape(step, tile, hid)
+        act_v[part] = (v * half).astype(BF16).reshape(step, tile, hid)
         slope = half + (0.5 * v) * (1.0 - t * t) * (c0 * (1.0 + 3.0 * 0.044715 * v2))
         grad_pre = (gout_v[part].reshape(step * tile, hid).astype(F32) * slope).astype(BF16)
         nt = (((1,), (1,)), ((), ()))
@@ -238,7 +245,8 @@
     mate = me + 1 - 2 * core
     pair = remote(gw.at[1 - core], from_core, core_send, core_recv, "rows", mate)
     pair.start()
-    work(groups + 1, 0)
+    act_out = pltpu.make_async_copy(act_v, act_hbm, gout_sem)
+    act_out.start()
 
     def share_copy(p, slot):
         return remote(stage.at[p], ret_hbm.at[slot], s_send.at[p], s_recv.at[slot], "rows", p)
@@ -278,6 +286,7 @@
         self_copy(p, mc).start()
     own_self = pltpu.make_async_copy(self_v.at[mc], selfp_hbm.at[mc], own_sem)
     own_self.start()
+    work(groups + 1, 0)
 
     def run(n, carry):
         last_slot, total = carry
@@ -320,7 +329,7 @@
         return remote(to_chip.at[q], from_chip.at[slot], chip_send.at[q], chip_recv.at[slot], "rows", 2 * q + core)
 
     over_chips(lambda q: chip_copy(q, chip).start())
-    shares(0, 8)
+    shares(0, 7)
     from_chip[chip] = to_chip[chip]
     over_chips(lambda q: chip_copy(q, q).wait())
     total = from_chip[0].astype(F32)
@@ -332,7 +341,7 @@
         return remote(sums.at[core, mc, chip], sums.at[core, mc, slot], up_send.at[q], up_recv.at[slot], "rows", 2 * q + core)
 
     over_chips(lambda q: up_copy(q, chip).start())
-    shares(8, 18)
+    shares(7, 14)
     over_chips(lambda q: up_copy(q, q).wait())
 
     def z_up(p, slot):
@@ -340,13 +349,15 @@
 
     for p in others():
         z_up(p, mc).start()
-    shares(18, parts - 1)
+    shares(14, parts - 1)
 
     def own_share(t, _):
-        own_ref[t] = share_of(t)
+        pool[t] = share_of(t)
         return 0
 
     lax.fori_loop(0, blocks, own_share, 0)
+    own_out = pltpu.make_async_copy(pool.at[pl.ds(0, blocks)], own_hbm, pool_sem)
+    own_out.start()
     for p in others():
         z_up(p, p).wait()
     pair_up = remote(sums.at[core], sums.at[core], pair_send, pair_recv, "rows", mate)
@@ -357,6 +368,8 @@
     for p in others():
         self_copy(p, p).wait()
     own_self.wait()
+    own_out.wait()
+    act_out.wait()
 
     def drain(d, _):
         p = lax.rem(me + d, parts)
@@ -407,8 +420,9 @@
             jax.ShapeDtypeStruct((parts * cap,), jnp.int32),
         ),
         in_specs=[VMEM, SMEM, VMEM, ANY, ANY, ANY, ANY, ANY],
-        out_specs=(VMEM, ANY, ANY, VMEM, VMEM, SMEM),
+        out_specs=(ANY, ANY, ANY, ANY, VMEM, SMEM),
         scratch_shapes=[
+            pltpu.VMEM(gout.shape, BF16),
             pltpu.VMEM((blocks + parts * cap, tile, width), BF16),
             pltpu.VMEM(feats.shape, BF16),
             pltpu.VMEM(adj.shape, BF16),
@@ -446,36 +460,62 @@
     )(fetch, colref, slots, feats, adj, w_self, w_neigh, gout)
 
 
-def combine_kernel(scale, wanted_ref, self_ref, own_ref, back_ref, sums_ref, act_ref,
-                   out_ref, gs_ref, gn_ref, act_out_ref, total):
-    slots = back_ref.shape[0]
-    act_out_ref[...] = act_ref[...]
-    total[...] = own_ref[...].astype(F32)
+def combine_kernel(scale, wanted_ref, self_hbm, own_hbm, back_hbm, sums_hbm, act_hbm,
+                   out_hbm, gs_hbm, gn_hbm, act_out_hbm,
+                   self_v, own_v, back_v, sums_v, out_v, weights, total, in_sem, out_sem):
+    moves = [
+        pltpu.make_async_copy(src, dst, in_sem.at[n])
+        for n, (src, dst) in enumerate(
+            ((own_hbm, own_v), (back_hbm, back_v), (sums_hbm, sums_v), (self_hbm, self_v), (act_hbm, act_out_hbm))
+        )
+    ]
+    for move in moves:
+        move.start()
+    moves[0].wait()
+    total[...] = own_v[...].astype(F32)
+    moves[1].wait()
 
     def add(s, _):
         t = wanted_ref[s]
 
         @pl.when(t >= 0)
         def _():
-            total[t] += back_ref[s].astype(F32)
-
-        return 0
-
-    lax.fori_loop(0, slots, add, 0)
-
-    def put(t, _):
-        out_ref[t] = self_ref[t].astype(F32) + total[t].T
-        return 0
-
-    lax.fori_loop(0, total.shape[0], put, 0, unroll=4)
-    halves, cols, chips, rows_p, cols_p = sums_ref.shape
-    hid = gs_ref.shape[0]
+            total[t] += back_v[s].astype(F32)
+
+        return 0
+
+    lax.fori_loop(0, back_v.shape[0], add, 0)
+    moves[2].wait()
+    halves, cols, chips, rows_p, cols_p = sums_v.shape
+    hid = weights.shape[1]
     wide = hid // cols_p
-    for half, ref in enumerate((gs_ref, gn_ref)):
+    for half in range(halves):
         for c in range(cols):
             for q in range(chips):
                 at = c * (hid // cols) + (q // wide) * rows_p
-                ref[at:at + rows_p, (q % wide) * cols_p:(q % wide + 1) * cols_p] = sums_ref[half, c, q].astype(F32) * scale
+                piece = sums_v[half, c, q].astype(F32) * scale
+                weights[half, at:at + rows_p, (q % wide) * cols_p:(q % wide + 1) * cols_p] = piece
+    done = [
+        pltpu.make_async_copy(weights.at[half], ref, out_sem.at[half]) for half, ref in enumerate((gs_hbm, gn_hbm))
+    ]
+    for move in done:
+        move.start()
+    moves[3].wait()
+    blocks = total.shape[0]
+    chunks = 4
+    size = blocks // chunks
+    for n in range(chunks):
+        def put(t, _):
+            out_v[t] = self_v[t].astype(F32) + total[t].T
+            return 0
+
+        lax.fori_loop(n * size, (n + 1) * size, put, 0, unroll=4)
+        part = pl.ds(n * size, size)
+        done.append(pltpu.make_async_copy(out_v.at[part], out_hbm.at[part], out_sem.at[halves + n]))
+        done[-1].start()
+    moves[4].wait()
+    for move in done:
+        move.wait()
 
 
 def combine(wanted, self_part, own, back, sums, act, scale):
@@ -484,10 +524,20 @@
     return pl.pallas_call(
         functools.partial(combine_kernel, scale),
         out_shape=(jax.ShapeDtypeStruct(self_part.shape, F32), weights, weights, jax.ShapeDtypeStruct(act.shape, BF16)),
-        in_specs=[SMEM, VMEM, VMEM, VMEM, VMEM, VMEM],
-        out_specs=(VMEM, VMEM, VMEM, VMEM),
-        scratch_shapes=[pltpu.VMEM(own.shape, F32)],
-        compiler_params=pltpu.CompilerParams(vmem_limit_bytes=40 << 20),
+        in_specs=[SMEM, ANY, ANY, ANY, ANY, ANY],
+        out_specs=(ANY, ANY, ANY, ANY),
+        scratch_shapes=[
+            pltpu.VMEM(self_part.shape, BF16),
+            pltpu.VMEM(own.shape, BF16),
+            pltpu.VMEM(back.shape, BF16),
+            pltpu.VMEM(sums.shape, BF16),
+            pltpu.VMEM(self_part.shape, F32),
+            pltpu.VMEM((2, hid, hid), F32),
+            pltpu.VMEM(own.shape, F32),
+            pltpu.SemaphoreType.DMA((5,)),
+            pltpu.SemaphoreType.DMA((6,)),
+        ],
+        compiler_params=pltpu.CompilerParams(vmem_limit_bytes=62 << 20),
         name="combine",
     )(wanted, self_part, own, back, sums, act)
 
@@ -504,7 +554,7 @@
     fetch = jnp.pad(fetch_ids.reshape(parts, cap).T, ((0, 0), (0, 128 - parts)))
     gout = grad_out.reshape(blocks // cols, tile, hid)
     act, self_part, returned, own, sums, wanted = layer(
-        fetch, colref.T, colref.reshape(1, refs), feats.reshape(blocks, tile, width),
+        fetch, colref.T, colref.T, feats.reshape(blocks, tile, width),
         adj_vals.reshape(refs, tile, tile), w_self, w_neigh, gout, parts, cols, cap,
     )
     grad_feats, grad_self, grad_neigh, act = combine(

time: 133 us -> 154 us (1.16)
  the two profiles are of different devices: /device:TPU:1 before, /device:TPU:19 now
where the time goes in v5:
time: 154 us
  Pallas kernels  152 us (99%)
    pallas_call x1, Pallas kernels, layer(): pl.pallas_call(functools.partial(layer_kernel, parts, cols, cap, blocks,...  119 us
    pallas_call x1, Pallas kernels, combine(): pl.pallas_call(functools.partial(combine_kernel, scale), out_shape=(jax.S...  33.6 us

profile of v5, /device:TPU:19, one launch (start us, length us, event | category | flops | bytes accessed | tf_op | source)
XLA Modules:
  0.0 154.2 jit_solution(12666520907366745051)
XLA Ops:
  0.6 1.2 pad.4.fetch_ref
  1.9 118.7 %layer.1 = (bf16[8,128,512]{2,1,0:T(8,128)(2,1)}, bf16[4,8,128,128]{3,2,1,0:T(8,128)(2,1)}, bf16[32,2,128,128]{3,2,1,0:T(8,128)(2,1)}, bf16[32,128,128]{2,1,0:T(...) custom-call(s32[2,128]{1,0:T(2,128)} %pad.4.fetch_ref, s32[16,32]{1,0:T(8,128)} %bitcast.16, ...), custom_call_target="tpu_custom_call" | custom-call | tf_op jit(solution)/shard_map/layer/pallas_call | solution.py:412
  120.6 33.6 %combine.1 = (f32[32,128,128]{2,1,0:T(8,128)}, f32[512,512]{1,0:T(8,128)}, f32[512,512]{1,0:T(8,128)}, bf16[8,128,512]{2,1,0:T(8,128)(2,1)}) custom-call(s32[64]{0:T(128)} %get-tuple-element.14.wanted_ref, bf16[32,128,128]{2,1,0:T(8,128)(2,1)} %bitcast.15, bf16[32,128,128]{2,1,0:T(8,128)(2,1)} %get-tuple-element.16.own_hbm, bf16[64,128,128]{2,1,0:T(8,128)(2,1)} %bitcast.12, ...), custom_call_target="tpu_custom_call" | custom-call | tf_op jit(solution)/shard_map/combine/pallas_call | solution.py:524

commit v6 on v5

--- a/solution.py
+++ b/solution.py
@@ -462,11 +462,11 @@
 
 def combine_kernel(scale, wanted_ref, self_hbm, own_hbm, back_hbm, sums_hbm, act_hbm,
                    out_hbm, gs_hbm, gn_hbm, act_out_hbm,
-                   self_v, own_v, back_v, sums_v, out_v, weights, total, in_sem, out_sem):
+                   self_v, own_v, back_v, sums_v, act_v, out_v, weights, total, in_sem, out_sem):
     moves = [
         pltpu.make_async_copy(src, dst, in_sem.at[n])
         for n, (src, dst) in enumerate(
-            ((own_hbm, own_v), (back_hbm, back_v), (sums_hbm, sums_v), (self_hbm, self_v), (act_hbm, act_out_hbm))
+            ((own_hbm, own_v), (back_hbm, back_v), (sums_hbm, sums_v), (self_hbm, self_v), (act_hbm, act_v))
         )
     ]
     for move in moves:
@@ -498,6 +498,8 @@
     done = [
         pltpu.make_async_copy(weights.at[half], ref, out_sem.at[half]) for half, ref in enumerate((gs_hbm, gn_hbm))
     ]
+    moves[4].wait()
+    done.append(pltpu.make_async_copy(act_v, act_out_hbm, out_sem.at[6]))
     for move in done:
         move.start()
     moves[3].wait()
@@ -513,7 +515,6 @@
         part = pl.ds(n * size, size)
         done.append(pltpu.make_async_copy(out_v.at[part], out_hbm.at[part], out_sem.at[halves + n]))
         done[-1].start()
-    moves[4].wait()
     for move in done:
         move.wait()
 
@@ -531,11 +532,12 @@
             pltpu.VMEM(own.shape, BF16),
             pltpu.VMEM(back.shape, BF16),
             pltpu.VMEM(sums.shape, BF16),
+            pltpu.VMEM(act.shape, BF16),
             pltpu.VMEM(self_part.shape, F32),
             pltpu.VMEM((2, hid, hid), F32),
             pltpu.VMEM(own.shape, F32),
             pltpu.SemaphoreType.DMA((5,)),
-            pltpu.SemaphoreType.DMA((6,)),
+            pltpu.SemaphoreType.DMA((7,)),
         ],
         compiler_params=pltpu.CompilerParams(vmem_limit_bytes=62 << 20),
         name="combine",

time: 154 us -> 127 us (0.82)
  Pallas kernels: 152 us -> 125 us
    pallas_call x1, Pallas kernels: 33.6 us -> 6.22 us  [combine(): pl.pallas_call(functools.partial(combine_kernel, scale), out_shape=(jax.S...]
where the time goes in v6:
time: 127 us
  Pallas kernels  125 us (98%)
    pallas_call x1, Pallas kernels, layer(): pl.pallas_call(functools.partial(layer_kernel, parts, cols, cap, blocks,...  119 us
    pallas_call x1, Pallas kernels, combine(): pl.pallas_call(functools.partial(combine_kernel, scale), out_shape=(jax.S...  6.22 us

profile of v6, /device:TPU:19, one launch (start us, length us, event | category | flops | bytes accessed | tf_op | source)
XLA Modules:
  0.0 126.8 jit_solution(10402576138276080938)
XLA Ops:
  0.6 1.2 pad.4.fetch_ref
  1.9 118.7 %layer.1 = (bf16[8,128,512]{2,1,0:T(8,128)(2,1)}, bf16[4,8,128,128]{3,2,1,0:T(8,128)(2,1)}, bf16[32,2,128,128]{3,2,1,0:T(8,128)(2,1)}, bf16[32,128,128]{2,1,0:T(...) custom-call(s32[2,128]{1,0:T(2,128)} %pad.4.fetch_ref, s32[16,32]{1,0:T(8,128)} %bitcast.16, ...), custom_call_target="tpu_custom_call" | custom-call | tf_op jit(solution)/shard_map/layer/pallas_call | solution.py:412
  120.6 6.2 %combine.1 = (f32[32,128,128]{2,1,0:T(8,128)}, f32[512,512]{1,0:T(8,128)}, f32[512,512]{1,0:T(8,128)}, bf16[8,128,512]{2,1,0:T(8,128)(2,1)}) custom-call(s32[64]{0:T(128)} %get-tuple-element.14.wanted_ref, bf16[32,128,128]{2,1,0:T(8,128)(2,1)} %bitcast.15, bf16[32,128,128]{2,1,0:T(8,128)(2,1)} %get-tuple-element.16.own_hbm, bf16[64,128,128]{2,1,0:T(8,128)(2,1)} %bitcast.12, ...), custom_call_target="tpu_custom_call" | custom-call | tf_op jit(solution)/shard_map/combine/pallas_call | solution.py:525
